TPU v7x, 32 devices: a whole 2x2x4 slice. The times are simulated.
32 devices in a mesh: clips: 2 (over y), ctx: 4 (over z), head: 4 (over x, core).
Axes of the slice: x: 2, y: 2, z: 4, core: 2. Of those that a mesh axis runs over, the one named last changes fastest.
Arguments:
- queries: bfloat16 [9216, 1536], P(('clips', 'ctx', 'head')), parts along dimension 0
- keys: bfloat16 [9216, 1536], P(('clips', 'ctx', 'head')), parts along dimension 0
- values: bfloat16 [9216, 1536], P(('clips', 'ctx', 'head')), parts along dimension 0, may hold values from -4.5 to 4.5
- neighbors: int32 [24, 8], P(('clips', 'ctx')), parts along dimension 0, may hold values from 0 to 11, as said below
- tile_counts: int32 [24], P(('clips', 'ctx')), parts along dimension 0, may hold values from 192 to 384
Outputs:
- attended: bfloat16 [9216, 1536], P(('clips', 'ctx', 'head')), parts along dimension 0
There are 2 independent parts, one for each index of `clips`. A program takes and returns all parts, laid end to end along the dimension named above; each array names one. Nothing has to cross between parts.
Inputs may be any that keep to these rules, and one draw needn't show every extreme that they name: `neighbors`: row t starts with t itself, followed by 8 - 1 distinct other tiles of t's 3 x 3 x 3 window of tiles: frame layer, row and column each differ from t's by at most one.
All inputs are finite; a program needn't handle non-finite values.
Results may differ from a plain program's by a relative error of at most 0.0049.
Values may be sent and summed in bfloat16 or wider, within the bound.
A program may use at most 64 MiB of HBM per device.

v0:
```python
import jax
import jax.numpy as jnp
from jax import lax
from jax.sharding import PartitionSpec as P

DH = 128
TILE = 384
NB = 8
REACH = 10
HOPS = 4


def shifted(array, axis, by):
    peers = lax.axis_size(axis)
    pairs = [(i, i + by) for i in range(peers) if 0 <= i + by < peers]
    return lax.ppermute(array, axis, pairs)


def join_pieces(pieces):
    return tuple(
        (jnp.concatenate([piece[member] for piece in pieces], axis=0) for member in range(3))
    )


def shards(queries, keys, values, neighbors, tile_counts):
    block_queries, block_keys, block_values = (
        lax.all_to_all(queries, "head", split_axis=1, concat_axis=0, tiled=True),
        lax.all_to_all(keys, "head", split_axis=1, concat_axis=0, tiled=True),
        lax.all_to_all(values, "head", split_axis=1, concat_axis=0, tiled=True),
    )
    tiles_here = tile_counts.shape[0]
    local_width = block_queries.shape[1]
    local_heads = local_width // DH
    earlier = []
    later = []
    for distance in range(1, HOPS + 1):
        taken = min(tiles_here, REACH - (distance - 1) * tiles_here)
        rows_taken = taken * TILE
        sent_back = (block_keys[-rows_taken:], block_values[-rows_taken:], tile_counts[-taken:])
        earlier = [shifted((sent_back[0], sent_back[1], sent_back[2]), "ctx", distance)] + earlier
        sent_fore = (block_keys[:rows_taken], block_values[:rows_taken], tile_counts[:taken])
        later = later + [shifted((sent_fore[0], sent_fore[1], sent_fore[2]), "ctx", -distance)]
    before = join_pieces(earlier)
    after = join_pieces(later)
    ext_tiles = tiles_here + 2 * REACH
    ext_keys = jnp.concatenate([before[0], block_keys, after[0]], axis=0).reshape(
        ext_tiles, TILE, local_width
    )
    ext_values = jnp.concatenate([before[1], block_values, after[1]], axis=0).reshape(
        ext_tiles, TILE, local_width
    )
    ext_counts = jnp.concatenate([before[2], tile_counts, after[2]], axis=0)
    slot_index = jnp.arange(TILE, dtype=jnp.int32)
    key_live = slot_index[None, :] < ext_counts[:, None]
    first_tile = lax.axis_index("ctx") * tiles_here - REACH
    local_lists = jnp.clip(neighbors - first_tile, 0, ext_tiles - 1)
    query_tiles = block_queries.reshape(tiles_here, TILE, local_width)

    def one_tile(tile_index):
        query_block = query_tiles[tile_index]
        listed = local_lists[tile_index]
        key_block = ext_keys[listed].reshape(NB * TILE, local_width)
        value_block = ext_values[listed].reshape(NB * TILE, local_width)
        key_mask = key_live[listed].reshape(NB * TILE)

        def one_head(head_index, result):
            start = head_index * DH
            query_rows = lax.dynamic_slice_in_dim(query_block, start, DH, 1)
            key_rows = lax.dynamic_slice_in_dim(key_block, start, DH, 1)
            value_rows = lax.dynamic_slice_in_dim(value_block, start, DH, 1)
            scores = lax.dot_general(
                query_rows, key_rows, (((1,), (1,)), ((), ())), preferred_element_type=jnp.float32
            ) * DH ** (-0.5)
            scores = jnp.where(key_mask[None, :], scores, -jnp.inf)
            highest = jnp.max(scores, axis=1, keepdims=True)
            weights = jnp.exp(scores - highest)
            totals = jnp.sum(weights, axis=1, keepdims=True)
            rounded = weights.astype(jnp.bfloat16)
            summed = jnp.dot(rounded, value_rows, preferred_element_type=jnp.float32)
            head_out = (summed / totals).astype(jnp.bfloat16)
            return lax.dynamic_update_slice_in_dim(result, head_out, start, 1)

        empty = jnp.zeros((TILE, local_width), jnp.bfloat16)
        return lax.fori_loop(0, local_heads, one_head, empty)

    outputs = lax.map(one_tile, jnp.arange(tiles_here, dtype=jnp.int32))
    outputs = outputs.reshape(tiles_here * TILE, local_width)
    return lax.all_to_all(outputs, "head", split_axis=0, concat_axis=1, tiled=True)


def solution(mesh):
    placed = (
        P(("clips", "ctx", "head"), None),
        P(("clips", "ctx", "head"), None),
        P(("clips", "ctx", "head"), None),
        P(("clips", "ctx"), None),
        P(("clips", "ctx")),
    )
    return jax.shard_map(
        shards,
        mesh=mesh,
        in_specs=placed,
        out_specs=P(("clips", "ctx", "head"), None),
        check_vma=False,
    )
```

profile of v0, /device:TPU:0, one launch (start us, length us, event | category | flops | bytes accessed | tf_op | source)
XLA Modules:
  0.0 357.6 jit_solution(14620852755360953468)
XLA Ops:
  0.0 2.2 copy.22
  2.3 4.2 %all-to-all-start.2 = ((bf16[288,4,384]{2,0,1:T(8,128)(2,1)}), bf16[288,4,384]{2,0,1:T(8,128)(2,1)S(1)}, u32[]{:S(2)}, u32[]{:S(2)}) async-start(bf16[288,4,384]{2,0,1:T(8,128)(2,1)} %bitcast.39), calls=%async_computation.2 | async-start | bytes 1769472 | tf_op jit(solution)/shard_map/all_to_all | solution.py:29
  6.5 2.2 copy.23
  8.7 10.5 %all-to-all-done.2 = bf16[288,4,384]{2,0,1:T(8,128)(2,1)S(1)} async-done(((bf16[288,4,384]{2,0,1:T(8,128)(2,1)}), bf16[288,4,384]{2,0,1:T(8,128)(2,1)S(1)}, u32[]{:S(2)}, u32[]{:S(2)}) %all-to-all-start.2) | async-done | bytes 884768 | tf_op jit(solution)/shard_map/all_to_all | solution.py:29
  19.2 3.5 all-to-all-start.1
  22.7 6.2 %collective-permute-start.17 = (s32[3]{0:T(128)S(1)}, s32[3]{0:T(128)S(1)}, u32[]{:S(2)}, u32[]{:S(2)}) collective-permute-start(s32[3]{0:T(128)S(1)} %copy-done.4), channel_id=1, source_target_pairs={{0,12},{1,13},{2,14},{3,15},{16,28},{17,29},{18,30},{19,31}} | collective-permute-start | bytes 44 | tf_op jit(solution)/shard_map/ppermute | solution.py:16
  35.3 1.4 collective-permute-start.8
  36.7 4.2 %all-to-all-start = ((bf16[288,4,384]{2,0,1:T(8,128)(2,1)}), bf16[288,4,384]{2,0,1:T(8,128)(2,1)}, u32[]{:S(2)}, u32[]{:S(2)}) async-start(bf16[288,4,384]{2,0,1:T(8,128)(2,1)} %bitcast.41), calls=%async_computation | async-start | bytes 1769472 | tf_op jit(solution)/shard_map/all_to_all | solution.py:27
  43.1 3.8 %collective-permute-start.18 = (s32[3]{0:T(128)S(1)}, s32[3]{0:T(128)S(1)}, u32[]{:S(2)}, u32[]{:S(2)}) collective-permute-start(s32[3]{0:T(128)S(1)} %copy-done.4), channel_id=1, source_target_pairs={{0,8},{4,12},{1,9},{5,13},{2,10},{6,14},{3,11},{7,15},{16,24},{20,... | collective-permute-start | bytes 44 | tf_op jit(solution)/shard_map/ppermute | solution.py:16
  46.9 3.5 collective-permute-start.19
  50.4 21.2 %collective-permute-done.18 = s32[3]{0:T(128)S(1)} collective-permute-done((s32[3]{0:T(128)S(1)}, s32[3]{0:T(128)S(1)}, u32[]{:S(2)}, u32[]{:S(2)}) %collective-permute-start.18) | collective-permute-done | bytes 44 | tf_op jit(solution)/shard_map/ppermute | solution.py:16
  74.2 21.3 %collective-permute-done.20 = s32[3]{0:T(128)S(1)} collective-permute-done((s32[3]{0:T(128)S(1)}, s32[3]{0:T(128)S(1)}, u32[]{:S(2)}, u32[]{:S(2)}) %collective-permute-start.20) | collective-permute-done | bytes 44 | tf_op jit(solution)/shard_map/ppermute | solution.py:16
  96.8 1.5 collective-permute-done.21
  98.2 4.9 %collective-permute-start.11 = (bf16[1152,384]{1,0:T(8,128)(2,1)S(1)}, bf16[1152,384]{1,0:T(8,128)(2,1)}, u32[]{:S(2)}, u32[]{:S(2)}) collective-permute-start(bf16[1152,384]{1,0:T(8,128)(2,1)S(1)} %bitcast.69), channel_id=1, source_target_pairs={{0,4},{4,8},{8,12},{1,5},{5,9},{9,13},{2,6},{6,10},{10,14},{3,7},{... | collective-permute-start | bytes 2654216 | tf_op jit(solution)/shard_map/ppermute | solution.py:16
  103.7 1.4 collective-permute-start
  105.1 2.1 concatenate.11
  108.4 1.7 constant_dynamic-update-slice_fusion.17
  111.4 1.7 constant_dynamic-update-slice_fusion.8
  113.1 7.6 %collective-permute-start.1 = (bf16[1152,384]{1,0:T(8,128)(2,1)S(1)}, bf16[1152,384]{1,0:T(8,128)(2,1)S(1)}, u32[]{:S(2)}, u32[]{:S(2)}) collective-permute-start(bf16[1152,384]{1,0:T(8,128)(2,1)S(1)} %bitcast.59), channel_id=1, source_target_pairs={{0,12},{1,13},{2,14},{3,15},{16,28},{17,29},{18,30},{19,31}} | collective-permute-start | bytes 2654216 | tf_op jit(solution)/shard_map/ppermute | solution.py:16
  121.8 1.5 collective-permute-start.2
  124.4 2.6 collective-permute-start.3
  127.0 2.2 constant_dynamic-update-slice_fusion.14
  130.1 10.6 %collective-permute-done.1 = bf16[1152,384]{1,0:T(8,128)(2,1)S(1)} collective-permute-done((bf16[1152,384]{1,0:T(8,128)(2,1)S(1)}, bf16[1152,384]{1,0:T(8,128)(2,1)S(1)}, u32[]{:S(2)}, u32[]{:S(2)}) %collective-permute-start.1) | collective-permute-done | bytes 884768 | tf_op jit(solution)/shard_map/ppermute | solution.py:16
  143.1 16.6 %collective-permute-done.2 = bf16[1152,384]{1,0:T(8,128)(2,1)S(1)} collective-permute-done((bf16[1152,384]{1,0:T(8,128)(2,1)S(1)}, bf16[1152,384]{1,0:T(8,128)(2,1)S(1)}, u32[]{:S(2)}, u32[]{:S(2)}) %collective-permute-start.2) | collective-permute-done | bytes 884768 | tf_op jit(solution)/shard_map/ppermute | solution.py:16
  162.0 15.1 %collective-permute-done.3 = bf16[1152,384]{1,0:T(8,128)(2,1)S(1)} collective-permute-done((bf16[1152,384]{1,0:T(8,128)(2,1)S(1)}, bf16[1152,384]{1,0:T(8,128)(2,1)S(1)}, u32[]{:S(2)}, u32[]{:S(2)}) %collective-permute-start.3) | collective-permute-done | bytes 884768 | tf_op jit(solution)/shard_map/ppermute | solution.py:16
  182.7 4.3 %collective-permute-done.13 = bf16[1152,384]{1,0:T(8,128)(2,1)S(1)} collective-permute-done((bf16[1152,384]{1,0:T(8,128)(2,1)S(1)}, bf16[1152,384]{1,0:T(8,128)(2,1)S(1)}, u32[]{:S(2)}, u32[]{:S(2)}) %collective-permute-start.13) | collective-permute-done | bytes 884768 | tf_op jit(solution)/shard_map/ppermute | solution.py:16
  190.4 13.4 %collective-permute-done.4 = bf16[1152,384]{1,0:T(8,128)(2,1)S(1)} collective-permute-done((bf16[1152,384]{1,0:T(8,128)(2,1)S(1)}, bf16[1152,384]{1,0:T(8,128)(2,1)S(1)}, u32[]{:S(2)}, u32[]{:S(2)}) %collective-permute-start.4) | collective-permute-done | bytes 884768 | tf_op jit(solution)/shard_map/ppermute | solution.py:16
  204.8 55.9 %collective-permute-done.5 = bf16[1152,384]{1,0:T(8,128)(2,1)S(1)} collective-permute-done((bf16[1152,384]{1,0:T(8,128)(2,1)S(1)}, bf16[1152,384]{1,0:T(8,128)(2,1)S(1)}, u32[]{:S(2)}, u32[]{:S(2)}) %collective-permute-start.5) | collective-permute-done | bytes 884768 | tf_op jit(solution)/shard_map/ppermute | solution.py:16
  264.3 76.2 %while.27 = (s32[]{:T(128)}, bf16[3,384,384]{2,1,0:T(8,128)(2,1)}, s32[3]{0:T(128)S(1)}, bf16[3,384,384]{2,1,0:T(8,128)(2,1)}, s32[3,8]{1,0:T(4,128)S(1)}, /*ind...) while((s32[]{:T(128)}, bf16[3,384,384]{2,1,0:T(8,128)(2,1)}, ...), condition=%wide.region_5.6_spmd.clone, body=%wide.region_0.5_spmd.clone.sunk | while | flops 612344704 | bytes 26889600 | solution.py:86
  267.5 4.0 %gather_fusion.1 = bf16[8,384,384]{2,1,0:T(8,128)(2,1)S(1)} fusion(bf16[23,384,384]{2,1,0:T(8,128)(2,1)} %get-tuple-element.422, s32[1024]{0:T(1024)S(1)} %pad_clamp_fusion.2), kind=kCustom, calls=%fused_computation.1.clone.clone.1 | custom fusion | bytes 4718624 | tf_op jit(solution)/shard_map/while/body/eval_jaxpr/gather | solution.py:62
  271.5 5.2 %gather_fusion.2 = bf16[8,384,384]{2,1,0:T(8,128)(2,1)} fusion(bf16[23,384,384]{2,1,0:T(8,128)(2,1)} %get-tuple-element.423, s32[1024]{0:T(1024)S(1)} %pad_clamp_fusion.2), kind=kCustom, calls=%fused_computation.2.clone.clone.1 | custom fusion | bytes 4718624 | tf_op jit(solution)/shard_map/while/body/eval_jaxpr/gather | solution.py:63
  277.7 11.2 %while.28 = (s32[]{:T(128)}, bf16[384,384]{1,0:T(8,128)(2,1)S(1)}, pred[8,384]{1,0:T(8,128)(4,1)}, bf16[384,384]{1,0:T(8,128)(2,1)S(1)}, bf16[3072,384]{1,0:T(8,...) while((s32[]{:T(128)}, bf16[384,384]{1,0:T(8,128)(2,1)S(1)}, ...), condition=%wide.wide.region_4.4_spmd, body=%wide.wide.region_1.3_spmd.sunk | while | flops 612334848 | bytes 15939227 | solution.py:84
  279.4 2.0 fusion.43
  283.2 2.0 fusion.43
  286.9 2.0 fusion.43
  292.9 4.0 %gather_fusion.1 = bf16[8,384,384]{2,1,0:T(8,128)(2,1)S(1)} fusion(bf16[23,384,384]{2,1,0:T(8,128)(2,1)} %get-tuple-element.422, s32[1024]{0:T(1024)S(1)} %pad_clamp_fusion.2), kind=kCustom, calls=%fused_computation.1.clone.clone.1 | custom fusion | bytes 4718624 | tf_op jit(solution)/shard_map/while/body/eval_jaxpr/gather | solution.py:62
  296.8 5.2 %gather_fusion.2 = bf16[8,384,384]{2,1,0:T(8,128)(2,1)} fusion(bf16[23,384,384]{2,1,0:T(8,128)(2,1)} %get-tuple-element.423, s32[1024]{0:T(1024)S(1)} %pad_clamp_fusion.2), kind=kCustom, calls=%fused_computation.2.clone.clone.1 | custom fusion | bytes 4718624 | tf_op jit(solution)/shard_map/while/body/eval_jaxpr/gather | solution.py:63
  303.1 11.2 %while.28 = (s32[]{:T(128)}, bf16[384,384]{1,0:T(8,128)(2,1)S(1)}, pred[8,384]{1,0:T(8,128)(4,1)}, bf16[384,384]{1,0:T(8,128)(2,1)S(1)}, bf16[3072,384]{1,0:T(8,...) while((s32[]{:T(128)}, bf16[384,384]{1,0:T(8,128)(2,1)S(1)}, ...), condition=%wide.wide.region_4.4_spmd, body=%wide.wide.region_1.3_spmd.sunk | while | flops 612334848 | bytes 15939227 | solution.py:84
  304.8 2.0 fusion.43
  308.5 2.0 fusion.43
  312.3 2.0 fusion.43
  318.2 4.0 %gather_fusion.1 = bf16[8,384,384]{2,1,0:T(8,128)(2,1)S(1)} fusion(bf16[23,384,384]{2,1,0:T(8,128)(2,1)} %get-tuple-element.422, s32[1024]{0:T(1024)S(1)} %pad_clamp_fusion.2), kind=kCustom, calls=%fused_computation.1.clone.clone.1 | custom fusion | bytes 4718624 | tf_op jit(solution)/shard_map/while/body/eval_jaxpr/gather | solution.py:62
  322.2 5.2 %gather_fusion.2 = bf16[8,384,384]{2,1,0:T(8,128)(2,1)} fusion(bf16[23,384,384]{2,1,0:T(8,128)(2,1)} %get-tuple-element.423, s32[1024]{0:T(1024)S(1)} %pad_clamp_fusion.2), kind=kCustom, calls=%fused_computation.2.clone.clone.1 | custom fusion | bytes 4718624 | tf_op jit(solution)/shard_map/while/body/eval_jaxpr/gather | solution.py:63
  328.5 11.2 %while.28 = (s32[]{:T(128)}, bf16[384,384]{1,0:T(8,128)(2,1)S(1)}, pred[8,384]{1,0:T(8,128)(4,1)}, bf16[384,384]{1,0:T(8,128)(2,1)S(1)}, bf16[3072,384]{1,0:T(8,...) while((s32[]{:T(128)}, bf16[384,384]{1,0:T(8,128)(2,1)S(1)}, ...), condition=%wide.wide.region_4.4_spmd, body=%wide.wide.region_1.3_spmd.sunk | while | flops 612334848 | bytes 15939227 | solution.py:84
  330.2 2.0 fusion.43
  333.9 2.0 fusion.43
  337.7 2.0 fusion.43
  340.5 16.1 %all_to_all.73 = bf16[4,288,384]{2,1,0:T(8,128)(2,1)S(1)} all-to-all(bf16[4,288,384]{2,1,0:T(8,128)(2,1)} %bitcast.78), channel_id=1, replica_groups=mesh['clips'=2,'ctx'=4,'head'=4] {'head'}, dimensions={0} | all-to-all | bytes 1769472 | tf_op jit(solution)/shard_map/all_to_all | solution.py:88
  (126 shorter events, 62.1 us)
Async XLA Ops:
  0.0 22.7 %copy-start.4 = (s32[3]{0:T(128)S(1)}, s32[3]{0:T(128)}, u32[]{:S(2)}) copy-start(s32[3]{0:T(128)} %param.13) | copy-start | bytes 40
  0.0 30.7 %copy-start = (bf16[288,1536]{1,0:T(8,128)(2,1)S(1)}, bf16[288,1536]{1,0:T(8,128)(2,1)}, u32[]{:S(2)}) copy-start(bf16[288,1536]{1,0:T(8,128)(2,1)} %param.9) | copy-start | bytes 2654212
  0.0 105.1 %copy-start.5 = (s32[3,8]{1,0:T(4,128)S(1)}, s32[3,8]{1,0:T(4,128)}, u32[]{:S(2)}) copy-start(s32[3,8]{1,0:T(4,128)} %param.12) | copy-start | bytes 292
  2.3 16.9 %all-to-all-start.2 = ((bf16[288,4,384]{2,0,1:T(8,128)(2,1)}), bf16[288,4,384]{2,0,1:T(8,128)(2,1)S(1)}, u32[]{:S(2)}, u32[]{:S(2)}) async-start(bf16[288,4,384]{2,0,1:T(8,128)(2,1)} %bitcast.39), calls=%async_computation.2 | async-start | bytes 1769472 | tf_op jit(solution)/shard_map/all_to_all | solution.py:29
  19.2 17.5 %all-to-all-start.1 = ((bf16[288,4,384]{2,0,1:T(8,128)(2,1)}), bf16[288,4,384]{2,0,1:T(8,128)(2,1)S(1)}, u32[]{:S(2)}, u32[]{:S(2)}) async-start(bf16[288,4,384]{2,0,1:T(8,128)(2,1)} %bitcast.40), calls=%async_computation.1 | async-start | bytes 1769472 | tf_op jit(solution)/shard_map/all_to_all | solution.py:28
  22.7 24.2 %collective-permute-start.17 = (s32[3]{0:T(128)S(1)}, s32[3]{0:T(128)S(1)}, u32[]{:S(2)}, u32[]{:S(2)}) collective-permute-start(s32[3]{0:T(128)S(1)} %copy-done.4), channel_id=1, source_target_pairs={{0,12},{1,13},{2,14},{3,15},{16,28},{17,29},{18,30},{19,31}} | collective-permute-start | bytes 44 | tf_op jit(solution)/shard_map/ppermute | solution.py:16
  29.5 12.3 %collective-permute-start.16 = (s32[1]{0:T(128)}, s32[1]{0:T(128)}, u32[]{:S(2)}, u32[]{:S(2)}) collective-permute-start(s32[1]{0:T(128)} %get-tuple-element.212), channel_id=1, source_target_pairs={} | collective-permute-start | bytes 20 | tf_op jit(solution)/shard_map/ppermute | solution.py:16
  31.8 81.4 %collective-permute-start.9 = (bf16[1152,384]{1,0:T(8,128)(2,1)S(1)}, bf16[1152,384]{1,0:T(8,128)(2,1)S(1)}, u32[]{:S(2)}, u32[]{:S(2)}) collective-permute-start(bf16[1152,384]{1,0:T(8,128)(2,1)S(1)} %bitcast.66), channel_id=1, source_target_pairs={{0,12},{1,13},{2,14},{3,15},{16,28},{17,29},{18,30},{19,31}} | collective-permute-start | bytes 2654216 | tf_op jit(solution)/shard_map/ppermute | solution.py:16
  33.1 88.7 %collective-permute-start.10 = (bf16[1152,384]{1,0:T(8,128)(2,1)S(1)}, bf16[1152,384]{1,0:T(8,128)(2,1)S(1)}, u32[]{:S(2)}, u32[]{:S(2)}) collective-permute-start(bf16[1152,384]{1,0:T(8,128)(2,1)S(1)} %bitcast.67), channel_id=1, source_target_pairs={{0,8},{4,12},{1,9},{5,13},{2,10},{6,14},{3,11},{7,15},{16,24},{20,... | collective-permute-start | bytes 2654216 | tf_op jit(solution)/shard_map/ppermute | solution.py:16
  35.3 71.8 %collective-permute-start.8 = (bf16[384,384]{1,0:T(8,128)(2,1)}, bf16[384,384]{1,0:T(8,128)(2,1)}, u32[]{:S(2)}, u32[]{:S(2)}) collective-permute-start(bf16[384,384]{1,0:T(8,128)(2,1)} %get-tuple-element.208), channel_id=1, source_target_pairs={} | collective-permute-start | bytes 884744 | tf_op jit(solution)/shard_map/ppermute | solution.py:16
  36.7 227.6 %all-to-all-start = ((bf16[288,4,384]{2,0,1:T(8,128)(2,1)}), bf16[288,4,384]{2,0,1:T(8,128)(2,1)}, u32[]{:S(2)}, u32[]{:S(2)}) async-start(bf16[288,4,384]{2,0,1:T(8,128)(2,1)} %bitcast.41), calls=%async_computation | async-start | bytes 1769472 | tf_op jit(solution)/shard_map/all_to_all | solution.py:27
  41.9 1.2 collective-permute-start.23
  43.1 28.5 %collective-permute-start.18 = (s32[3]{0:T(128)S(1)}, s32[3]{0:T(128)S(1)}, u32[]{:S(2)}, u32[]{:S(2)}) collective-permute-start(s32[3]{0:T(128)S(1)} %copy-done.4), channel_id=1, source_target_pairs={{0,8},{4,12},{1,9},{5,13},{2,10},{6,14},{3,11},{7,15},{16,24},{20,... | collective-permute-start | bytes 44 | tf_op jit(solution)/shard_map/ppermute | solution.py:16
  46.9 26.0 %collective-permute-start.19 = (s32[3]{0:T(128)S(1)}, s32[3]{0:T(128)S(1)}, u32[]{:S(2)}, u32[]{:S(2)}) collective-permute-start(s32[3]{0:T(128)S(1)} %copy-done.4), channel_id=1, source_target_pairs={{0,4},{4,8},{8,12},{1,5},{5,9},{9,13},{2,6},{6,10},{10,14},{3,7},{... | collective-permute-start | bytes 44 | tf_op jit(solution)/shard_map/ppermute | solution.py:16
  71.6 31.6 %copy-start.6 = (s32[3]{0:T(128)}, s32[3]{0:T(128)S(1)}, u32[]{:S(2)}) copy-start(s32[3]{0:T(128)S(1)} %collective-permute-done.18) | copy-start | bytes 40
  71.6 23.9 %collective-permute-start.20 = (s32[3]{0:T(128)S(1)}, s32[3]{0:T(128)S(1)}, u32[]{:S(2)}, u32[]{:S(2)}) collective-permute-start(s32[3]{0:T(128)S(1)} %copy-done.4), channel_id=1, source_target_pairs={{4,0},{8,4},{12,8},{5,1},{9,5},{13,9},{6,2},{10,6},{14,10},{7,3},{... | collective-permute-start | bytes 44 | tf_op jit(solution)/shard_map/ppermute | solution.py:16
  72.9 30.3 %copy-start.7 = (s32[3]{0:T(128)}, s32[3]{0:T(128)S(1)}, u32[]{:S(2)}) copy-start(s32[3]{0:T(128)S(1)} %collective-permute-done.19) | copy-start | bytes 40
  72.9 25.3 %collective-permute-start.21 = (s32[3]{0:T(128)S(1)}, s32[3]{0:T(128)S(1)}, u32[]{:S(2)}, u32[]{:S(2)}) collective-permute-start(s32[3]{0:T(128)S(1)} %copy-done.4), channel_id=1, source_target_pairs={{8,0},{12,4},{9,1},{13,5},{10,2},{14,6},{11,3},{15,7},{24,16},{28,... | collective-permute-start | bytes 44 | tf_op jit(solution)/shard_map/ppermute | solution.py:16
  95.5 7.7 %copy-start.8 = (s32[3]{0:T(128)}, s32[3]{0:T(128)S(1)}, u32[]{:S(2)}) copy-start(s32[3]{0:T(128)S(1)} %collective-permute-done.20) | copy-start | bytes 40
  95.5 7.7 %collective-permute-start.22 = (s32[3]{0:T(128)S(1)}, s32[3]{0:T(128)S(1)}, u32[]{:S(2)}, u32[]{:S(2)}) collective-permute-start(s32[3]{0:T(128)S(1)} %copy-done.4), channel_id=1, source_target_pairs={{12,0},{13,1},{14,2},{15,3},{28,16},{29,17},{30,18},{31,19}} | collective-permute-start | bytes 44 | tf_op jit(solution)/shard_map/ppermute | solution.py:16
  98.2 5.0 %copy-start.9 = (s32[3]{0:T(128)}, s32[3]{0:T(128)S(1)}, u32[]{:S(2)}) copy-start(s32[3]{0:T(128)S(1)} %collective-permute-done.21) | copy-start | bytes 40
  98.2 26.1 %collective-permute-start.11 = (bf16[1152,384]{1,0:T(8,128)(2,1)S(1)}, bf16[1152,384]{1,0:T(8,128)(2,1)}, u32[]{:S(2)}, u32[]{:S(2)}) collective-permute-start(bf16[1152,384]{1,0:T(8,128)(2,1)S(1)} %bitcast.69), channel_id=1, source_target_pairs={{0,4},{4,8},{8,12},{1,5},{5,9},{9,13},{2,6},{6,10},{10,14},{3,7},{... | collective-permute-start | bytes 2654216 | tf_op jit(solution)/shard_map/ppermute | solution.py:16
  103.2 0.5 copy-start.10
  103.7 6.4 %collective-permute-start = (bf16[384,384]{1,0:T(8,128)(2,1)}, bf16[384,384]{1,0:T(8,128)(2,1)}, u32[]{:S(2)}, u32[]{:S(2)}) collective-permute-start(bf16[384,384]{1,0:T(8,128)(2,1)} %get-tuple-element.210), channel_id=1, source_target_pairs={} | collective-permute-start | bytes 884744 | tf_op jit(solution)/shard_map/ppermute | solution.py:16
  107.1 73.3 %collective-permute-start.12 = (bf16[1152,384]{1,0:T(8,128)(2,1)S(1)}, bf16[1152,384]{1,0:T(8,128)(2,1)S(1)}, u32[]{:S(2)}, u32[]{:S(2)}) collective-permute-start(bf16[1152,384]{1,0:T(8,128)(2,1)S(1)} %bitcast.70), channel_id=1, source_target_pairs={{4,0},{8,4},{12,8},{5,1},{9,5},{13,9},{6,2},{10,6},{14,10},{7,3},{... | collective-permute-start | bytes 2654216 | tf_op jit(solution)/shard_map/ppermute | solution.py:16
  110.1 76.9 %collective-permute-start.13 = (bf16[1152,384]{1,0:T(8,128)(2,1)S(1)}, bf16[1152,384]{1,0:T(8,128)(2,1)S(1)}, u32[]{:S(2)}, u32[]{:S(2)}) collective-permute-start(bf16[1152,384]{1,0:T(8,128)(2,1)S(1)} %bitcast.71), channel_id=1, source_target_pairs={{8,0},{12,4},{9,1},{13,5},{10,2},{14,6},{11,3},{15,7},{24,16},{28,... | collective-permute-start | bytes 2654216 | tf_op jit(solution)/shard_map/ppermute | solution.py:16
  113.1 27.6 %collective-permute-start.1 = (bf16[1152,384]{1,0:T(8,128)(2,1)S(1)}, bf16[1152,384]{1,0:T(8,128)(2,1)S(1)}, u32[]{:S(2)}, u32[]{:S(2)}) collective-permute-start(bf16[1152,384]{1,0:T(8,128)(2,1)S(1)} %bitcast.59), channel_id=1, source_target_pairs={{0,12},{1,13},{2,14},{3,15},{16,28},{17,29},{18,30},{19,31}} | collective-permute-start | bytes 2654216 | tf_op jit(solution)/shard_map/ppermute | solution.py:16
  121.8 65.2 %copy-start.2 = (bf16[384,384]{1,0:T(8,128)(2,1)S(1)}, bf16[384,384]{1,0:T(8,128)(2,1)}, u32[]{:S(2)}) copy-start(bf16[384,384]{1,0:T(8,128)(2,1)} %get-tuple-element.207) | copy-start | bytes 884740
  121.8 37.9 %collective-permute-start.2 = (bf16[1152,384]{1,0:T(8,128)(2,1)S(1)}, bf16[1152,384]{1,0:T(8,128)(2,1)S(1)}, u32[]{:S(2)}, u32[]{:S(2)}) collective-permute-start(bf16[1152,384]{1,0:T(8,128)(2,1)S(1)} %bitcast.60), channel_id=1, source_target_pairs={{0,8},{4,12},{1,9},{5,13},{2,10},{6,14},{3,11},{7,15},{16,24},{20,... | collective-permute-start | bytes 2654216 | tf_op jit(solution)/shard_map/ppermute | solution.py:16
  124.4 64.3 %copy-start.3 = (bf16[384,384]{1,0:T(8,128)(2,1)S(1)}, bf16[384,384]{1,0:T(8,128)(2,1)}, u32[]{:S(2)}) copy-start(bf16[384,384]{1,0:T(8,128)(2,1)} %get-tuple-element.209) | copy-start | bytes 884740
  124.4 52.7 %collective-permute-start.3 = (bf16[1152,384]{1,0:T(8,128)(2,1)S(1)}, bf16[1152,384]{1,0:T(8,128)(2,1)S(1)}, u32[]{:S(2)}, u32[]{:S(2)}) collective-permute-start(bf16[1152,384]{1,0:T(8,128)(2,1)S(1)} %bitcast.61), channel_id=1, source_target_pairs={{0,4},{4,8},{8,12},{1,5},{5,9},{9,13},{2,6},{6,10},{10,14},{3,7},{... | collective-permute-start | bytes 2654216 | tf_op jit(solution)/shard_map/ppermute | solution.py:16
  140.8 47.9 %collective-permute-start.14 = (bf16[1152,384]{1,0:T(8,128)(2,1)S(1)}, bf16[1152,384]{1,0:T(8,128)(2,1)S(1)}, u32[]{:S(2)}, u32[]{:S(2)}) collective-permute-start(bf16[1152,384]{1,0:T(8,128)(2,1)S(1)} %bitcast.73), channel_id=1, source_target_pairs={{12,0},{13,1},{14,2},{15,3},{28,16},{29,17},{30,18},{31,19}} | collective-permute-start | bytes 2654216 | tf_op jit(solution)/shard_map/ppermute | solution.py:16
  159.7 44.1 %collective-permute-start.4 = (bf16[1152,384]{1,0:T(8,128)(2,1)S(1)}, bf16[1152,384]{1,0:T(8,128)(2,1)S(1)}, u32[]{:S(2)}, u32[]{:S(2)}) collective-permute-start(bf16[1152,384]{1,0:T(8,128)(2,1)S(1)} %bitcast.62), channel_id=1, source_target_pairs={{4,0},{8,4},{12,8},{5,1},{9,5},{13,9},{6,2},{10,6},{14,10},{7,3},{... | collective-permute-start | bytes 2654216 | tf_op jit(solution)/shard_map/ppermute | solution.py:16
  177.1 83.6 %collective-permute-start.5 = (bf16[1152,384]{1,0:T(8,128)(2,1)S(1)}, bf16[1152,384]{1,0:T(8,128)(2,1)S(1)}, u32[]{:S(2)}, u32[]{:S(2)}) collective-permute-start(bf16[1152,384]{1,0:T(8,128)(2,1)S(1)} %bitcast.63), channel_id=1, source_target_pairs={{8,0},{12,4},{9,1},{13,5},{10,2},{14,6},{11,3},{15,7},{24,16},{28,... | collective-permute-start | bytes 2654216 | tf_op jit(solution)/shard_map/ppermute | solution.py:16
  180.4 82.1 %collective-permute-start.6 = (bf16[1152,384]{1,0:T(8,128)(2,1)S(1)}, bf16[1152,384]{1,0:T(8,128)(2,1)S(1)}, u32[]{:S(2)}, u32[]{:S(2)}) collective-permute-start(bf16[1152,384]{1,0:T(8,128)(2,1)S(1)} %bitcast.65), channel_id=1, source_target_pairs={{12,0},{13,1},{14,2},{15,3},{28,16},{29,17},{30,18},{31,19}} | collective-permute-start | bytes 2654216 | tf_op jit(solution)/shard_map/ppermute | solution.py:16
  187.0 74.8 %collective-permute-start.15 = (bf16[384,384]{1,0:T(8,128)(2,1)S(1)}, bf16[384,384]{1,0:T(8,128)(2,1)S(1)}, u32[]{:S(2)}, u32[]{:S(2)}) collective-permute-start(bf16[384,384]{1,0:T(8,128)(2,1)S(1)} %copy-done.2), channel_id=1, source_target_pairs={} | collective-permute-start | bytes 884744 | tf_op jit(solution)/shard_map/ppermute | solution.py:16
  188.7 74.9 %collective-permute-start.7 = (bf16[384,384]{1,0:T(8,128)(2,1)S(1)}, bf16[384,384]{1,0:T(8,128)(2,1)S(1)}, u32[]{:S(2)}, u32[]{:S(2)}) collective-permute-start(bf16[384,384]{1,0:T(8,128)(2,1)S(1)} %copy-done.3), channel_id=1, source_target_pairs={} | collective-permute-start | bytes 884744 | tf_op jit(solution)/shard_map/ppermute | solution.py:16
  267.4 10.3 %copy-start.1 = (pred[8,384]{1,0:T(8,128)(4,1)}, pred[8,384]{1,0:T(8,128)(4,1)S(1)}, u32[]{:S(2)}) copy-start(pred[8,384]{1,0:T(8,128)(4,1)S(1)} %gather_fusion) | copy-start | bytes 9220 | tf_op jit(solution)/shard_map/while
  292.8 10.3 %copy-start.1 = (pred[8,384]{1,0:T(8,128)(4,1)}, pred[8,384]{1,0:T(8,128)(4,1)S(1)}, u32[]{:S(2)}) copy-start(pred[8,384]{1,0:T(8,128)(4,1)S(1)} %gather_fusion) | copy-start | bytes 9220 | tf_op jit(solution)/shard_map/while
  318.2 10.3 %copy-start.1 = (pred[8,384]{1,0:T(8,128)(4,1)}, pred[8,384]{1,0:T(8,128)(4,1)S(1)}, u32[]{:S(2)}) copy-start(pred[8,384]{1,0:T(8,128)(4,1)S(1)} %gather_fusion) | copy-start | bytes 9220 | tf_op jit(solution)/shard_map/while
where the time goes:
time: 359 us; the launch traced here: 358 us
  waiting for transfers between devices  170 us (47%)
  local copies, waits for them, and re-layouts  68.2 us (19%)
  starting transfers between devices  62.8 us (17%)
  matrix products  26.5 us (7%)
  blocking collectives  16.1 us (4%)
  other arithmetic  7.3 us (2%)
  loops' own time  5.99 us (2%)
    ppermute x24, waiting for transfers between devices, shifted(): return lax.ppermute(array, axis, pairs)  160 us
    ppermute x24, starting transfers between devices, shifted(): return lax.ppermute(array, axis, pairs)  50.8 us
    unnamed x36, local copies, waits for them, and re-layouts  19.4 us
    dot_general x9, matrix products, one_head(): summed = jnp.dot(rounded, value_rows, preferred_element_type=jnp.float32)  18.2 us
    all_to_all x1, blocking collectives, shards(): lax.all_to_all(outputs, 'head', split_axis=0, concat_axis=1, tiled=True)  16.1 us
    gather x3, local copies, waits for them, and re-layouts, one_tile(): value_block = ext_values[listed].reshape(NB * TILE, local_width)  15.6 us
    gather x3, local copies, waits for them, and re-layouts, one_tile(): key_block = ext_keys[listed].reshape(NB * TILE, local_width)  12 us
    all_to_all x1, waiting for transfers between devices, shards(): lax.all_to_all(values, 'head', split_axis=1, concat_axis=0, tiled=True)  10.5 us
  transfers between devices with their start and end apart: 27, of which 10 were waited for; matrix products, arithmetic and copies ran while one was open for 8% of the time, Pallas kernels for 0%

commit v1 on v0

--- a/solution.py
+++ b/solution.py
@@ -2,6 +2,8 @@
 import jax.numpy as jnp
 from jax import lax
 from jax.sharding import PartitionSpec as P
+from jax.experimental import pallas as pl
+from jax.experimental.pallas import tpu as pltpu
 
 DH = 128
 TILE = 384
@@ -20,6 +22,60 @@
     return tuple(
         (jnp.concatenate([piece[member] for piece in pieces], axis=0) for member in range(3))
     )
+
+
+def attend_kernel(lists_ref, counts_ref, query_ref, *refs):
+    key_refs = refs[:NB]
+    value_refs = refs[NB : 2 * NB]
+    out_ref = refs[2 * NB]
+    tile = pl.program_id(0)
+    query_rows = query_ref[...]
+    slot_index = lax.broadcasted_iota(jnp.int32, (TILE, TILE), 1)
+    scores = []
+    for entry in range(NB):
+        part = lax.dot_general(
+            query_rows, key_refs[entry][...], (((1,), (1,)), ((), ())),
+            preferred_element_type=jnp.float32,
+        ) * DH ** (-0.5)
+        live = slot_index < counts_ref[lists_ref[tile, entry]]
+        scores.append(jnp.where(live, part, -jnp.inf))
+    highest = scores[0].max(axis=1, keepdims=True)
+    for part in scores[1:]:
+        highest = jnp.maximum(highest, part.max(axis=1, keepdims=True))
+    totals = jnp.zeros((TILE, 1), jnp.float32)
+    summed = jnp.zeros((TILE, DH), jnp.float32)
+    for entry in range(NB):
+        weights = jnp.exp(scores[entry] - highest)
+        totals = totals + weights.sum(axis=1, keepdims=True)
+        summed = summed + jnp.dot(
+            weights.astype(jnp.bfloat16), value_refs[entry][...],
+            preferred_element_type=jnp.float32,
+        )
+    out_ref[...] = (summed / totals).astype(out_ref.dtype)
+
+
+def attend(local_lists, ext_counts, query_tiles, ext_keys, ext_values):
+    tiles_here, _, local_width = query_tiles.shape
+    local_heads = local_width // DH
+    own = pl.BlockSpec((None, TILE, DH), lambda t, h, lists, counts: (t, 0, h))
+
+    def listed(entry):
+        return pl.BlockSpec(
+            (None, TILE, DH), lambda t, h, lists, counts: (lists[t, entry], 0, h)
+        )
+
+    spec = pltpu.PrefetchScalarGridSpec(
+        num_scalar_prefetch=2,
+        grid=(tiles_here, local_heads),
+        in_specs=[own] + [listed(e) for e in range(NB)] * 2,
+        out_specs=own,
+    )
+    return pl.pallas_call(
+        attend_kernel,
+        grid_spec=spec,
+        out_shape=jax.ShapeDtypeStruct(query_tiles.shape, query_tiles.dtype),
+        compiler_params=pltpu.CompilerParams(vmem_limit_bytes=48 * 1024 * 1024),
+    )(local_lists, ext_counts, query_tiles, *([ext_keys] * NB), *([ext_values] * NB))
 
 
 def shards(queries, keys, values, neighbors, tile_counts):
@@ -50,40 +106,10 @@
         ext_tiles, TILE, local_width
     )
     ext_counts = jnp.concatenate([before[2], tile_counts, after[2]], axis=0)
-    slot_index = jnp.arange(TILE, dtype=jnp.int32)
-    key_live = slot_index[None, :] < ext_counts[:, None]
     first_tile = lax.axis_index("ctx") * tiles_here - REACH
-    local_lists = jnp.clip(neighbors - first_tile, 0, ext_tiles - 1)
+    local_lists = jnp.clip(neighbors - first_tile, 0, ext_tiles - 1).astype(jnp.int32)
     query_tiles = block_queries.reshape(tiles_here, TILE, local_width)
-
-    def one_tile(tile_index):
-        query_block = query_tiles[tile_index]
-        listed = local_lists[tile_index]
-        key_block = ext_keys[listed].reshape(NB * TILE, local_width)
-        value_block = ext_values[listed].reshape(NB * TILE, local_width)
-        key_mask = key_live[listed].reshape(NB * TILE)
-
-        def one_head(head_index, result):
-            start = head_index * DH
-            query_rows = lax.dynamic_slice_in_dim(query_block, start, DH, 1)
-            key_rows = lax.dynamic_slice_in_dim(key_block, start, DH, 1)
-            value_rows = lax.dynamic_slice_in_dim(value_block, start, DH, 1)
-            scores = lax.dot_general(
-                query_rows, key_rows, (((1,), (1,)), ((), ())), preferred_element_type=jnp.float32
-            ) * DH ** (-0.5)
-            scores = jnp.where(key_mask[None, :], scores, -jnp.inf)
-            highest = jnp.max(scores, axis=1, keepdims=True)
-            weights = jnp.exp(scores - highest)
-            totals = jnp.sum(weights, axis=1, keepdims=True)
-            rounded = weights.astype(jnp.bfloat16)
-            summed = jnp.dot(rounded, value_rows, preferred_element_type=jnp.float32)
-            head_out = (summed / totals).astype(jnp.bfloat16)
-            return lax.dynamic_update_slice_in_dim(result, head_out, start, 1)
-
-        empty = jnp.zeros((TILE, local_width), jnp.bfloat16)
-        return lax.fori_loop(0, local_heads, one_head, empty)
-
-    outputs = lax.map(one_tile, jnp.arange(tiles_here, dtype=jnp.int32))
+    outputs = attend(local_lists, ext_counts.astype(jnp.int32), query_tiles, ext_keys, ext_values)
     outputs = outputs.reshape(tiles_here * TILE, local_width)
     return lax.all_to_all(outputs, "head", split_axis=0, concat_axis=1, tiled=True)
 

time: 359 us -> 306 us (0.85)
  local copies, waits for them, and re-layouts: 68.2 us -> 27.6 us
  matrix products: 26.5 us -> 0 us
  Pallas kernels: 0 us -> 22.9 us
  other arithmetic: 7.3 us -> 0.01 us
  loops' own time: 5.99 us -> 0 us
  waiting for transfers between devices: 170 us -> 175 us
    gather x9 -> x0, local copies, waits for them, and re-layouts: 29.3 us -> none  [the longest x3 15.6 us: one_tile(): value_block = ext_values[listed].reshape(NB * TILE, local_width)]
    dot_general x18 -> x0, matrix products: 26.5 us -> none  [the longest x9 18.2 us: one_head(): summed = jnp.dot(rounded, value_rows, preferred_element_type=jnp.float32)]
    pallas_call x0 -> x1, Pallas kernels: none -> 22.9 us  [attend(): pl.pallas_call(attend_kernel, grid_spec=spec, out_shape=jax.ShapeDtypeStr...]
    reduce_sum x9 -> x0, other arithmetic: 7.02 us -> none  [one_head(): totals = jnp.sum(weights, axis=1, keepdims=True)]
    another operation x4 -> x0, loops' own time: 5.99 us -> none  [the longest x1 5.77 us: shards(): outputs = lax.map(one_tile, jnp.arange(tiles_here, dtype=jnp.int32))]
    ppermute x24, waiting for transfers between devices: 160 us -> 165 us  [shifted(): return lax.ppermute(array, axis, pairs)]
    unnamed x36 -> x38, local copies, waits for them, and re-layouts: 19.4 us -> 16.1 us
  transfers between devices with their start and end apart: 27 -> 27, of which waited for: 10 -> 10; matrix products, arithmetic and copies ran while one was open for 8% -> 7% of each run, Pallas kernels for 0% -> 0%
where the time goes in v1:
time: 306 us; the launch traced here: 305 us
  waiting for transfers between devices  175 us (57%)
  starting transfers between devices  63.2 us (21%)
  local copies, waits for them, and re-layouts  27.6 us (9%)
  Pallas kernels  22.9 us (7%)
  blocking collectives  15.3 us (5%)
    ppermute x24, waiting for transfers between devices, shifted(): return lax.ppermute(array, axis, pairs)  165 us
    ppermute x24, starting transfers between devices, shifted(): return lax.ppermute(array, axis, pairs)  52 us
    pallas_call x1, Pallas kernels, attend(): pl.pallas_call(attend_kernel, grid_spec=spec, out_shape=jax.ShapeDtypeStr...  22.9 us
    unnamed x38, local copies, waits for them, and re-layouts  16.1 us
    all_to_all x1, blocking collectives, shards(): lax.all_to_all(outputs, 'head', split_axis=0, concat_axis=1, tiled=True)  15.3 us
    all_to_all x1, waiting for transfers between devices, shards(): lax.all_to_all(values, 'head', split_axis=1, concat_axis=0, tiled=True)  10.5 us
  transfers between devices with their start and end apart: 27, of which 10 were waited for; matrix products, arithmetic and copies ran while one was open for 7% of the time, Pallas kernels for 0%

profile of v1, /device:TPU:0, one launch (start us, length us, event | category | flops | bytes accessed | tf_op | source)
XLA Modules:
  0.0 304.7 jit_solution(6292571730764101340)
XLA Ops:
  0.0 2.2 copy.23
  2.3 4.2 %all-to-all-start.2 = ((bf16[288,4,384]{2,0,1:T(8,128)(2,1)}), bf16[288,4,384]{2,0,1:T(8,128)(2,1)S(1)}, u32[]{:S(2)}, u32[]{:S(2)}) async-start(bf16[288,4,384]{2,0,1:T(8,128)(2,1)} %bitcast.24), calls=%async_computation.2 | async-start | bytes 1769472 | tf_op jit(solution)/shard_map/all_to_all | solution.py:85
  6.5 2.2 copy.24
  8.7 10.5 %all-to-all-done.2 = bf16[288,4,384]{2,0,1:T(8,128)(2,1)S(1)} async-done(((bf16[288,4,384]{2,0,1:T(8,128)(2,1)}), bf16[288,4,384]{2,0,1:T(8,128)(2,1)S(1)}, u32[]{:S(2)}, u32[]{:S(2)}) %all-to-all-start.2) | async-done | bytes 884768 | tf_op jit(solution)/shard_map/all_to_all | solution.py:85
  19.2 3.5 %all-to-all-start.1 = ((bf16[288,4,384]{2,0,1:T(8,128)(2,1)}), bf16[288,4,384]{2,0,1:T(8,128)(2,1)S(1)}, u32[]{:S(2)}, u32[]{:S(2)}) async-start(bf16[288,4,384]{2,0,1:T(8,128)(2,1)} %bitcast.25), calls=%async_computation.1 | async-start | bytes 1769472 | tf_op jit(solution)/shard_map/all_to_all | solution.py:84
  22.7 6.2 %collective-permute-start.1 = (s32[3]{0:T(128)S(1)}, s32[3]{0:T(128)S(1)}, u32[]{:S(2)}, u32[]{:S(2)}) collective-permute-start(s32[3]{0:T(128)S(1)} %copy-done.4), channel_id=1, source_target_pairs={{0,12},{1,13},{2,14},{3,15},{16,28},{17,29},{18,30},{19,31}} | collective-permute-start | bytes 44 | tf_op jit(solution)/shard_map/ppermute | solution.py:18
  29.5 1.1 collective-permute-start
  31.7 2.2 collective-permute-start.17
  33.9 1.3 collective-permute-start.18
  36.1 1.4 collective-permute-start.16
  37.5 3.5 %all-to-all-start = ((bf16[288,4,384]{2,0,1:T(8,128)(2,1)}), bf16[288,4,384]{2,0,1:T(8,128)(2,1)S(1)}, u32[]{:S(2)}, u32[]{:S(2)}) async-start(bf16[288,4,384]{2,0,1:T(8,128)(2,1)} %bitcast.26), calls=%async_computation | async-start | bytes 1769472 | tf_op jit(solution)/shard_map/all_to_all | solution.py:83
  41.9 1.2 collective-permute-start.7
  43.0 3.0 collective-permute-start.2
  46.1 3.5 %collective-permute-start.3 = (s32[3]{0:T(128)S(1)}, s32[3]{0:T(128)S(1)}, u32[]{:S(2)}, u32[]{:S(2)}) collective-permute-start(s32[3]{0:T(128)S(1)} %copy-done.4), channel_id=1, source_target_pairs={{0,4},{4,8},{8,12},{1,5},{5,9},{9,13},{2,6},{6,10},{10,14},{3,7},{... | collective-permute-start | bytes 44 | tf_op jit(solution)/shard_map/ppermute | solution.py:18
  49.6 21.9 %collective-permute-done.2 = s32[3]{0:T(128)S(1)} collective-permute-done((s32[3]{0:T(128)S(1)}, s32[3]{0:T(128)S(1)}, u32[]{:S(2)}, u32[]{:S(2)}) %collective-permute-start.2) | collective-permute-done | bytes 44 | tf_op jit(solution)/shard_map/ppermute | solution.py:18
  71.5 1.3 collective-permute-start.4
  72.8 1.3 collective-permute-start.5
  74.1 21.3 %collective-permute-done.4 = s32[3]{0:T(128)S(1)} collective-permute-done((s32[3]{0:T(128)S(1)}, s32[3]{0:T(128)S(1)}, u32[]{:S(2)}, u32[]{:S(2)}) %collective-permute-start.4) | collective-permute-done | bytes 44 | tf_op jit(solution)/shard_map/ppermute | solution.py:18
  95.4 1.3 collective-permute-start.6
  96.7 1.5 collective-permute-done.5
  98.2 5.0 %collective-permute-start.19 = (bf16[1152,384]{1,0:T(8,128)(2,1)S(1)}, bf16[1152,384]{1,0:T(8,128)(2,1)}, u32[]{:S(2)}, u32[]{:S(2)}) collective-permute-start(bf16[1152,384]{1,0:T(8,128)(2,1)S(1)} %bitcast.48), channel_id=1, source_target_pairs={{0,4},{4,8},{8,12},{1,5},{5,9},{9,13},{2,6},{6,10},{10,14},{3,7},{... | collective-permute-start | bytes 2654216 | tf_op jit(solution)/shard_map/ppermute | solution.py:18
  103.7 1.4 collective-permute-start.8
  105.1 1.9 concatenate.9.counts_ref
  107.0 1.3 collective-permute-start.20
  109.3 1.3 collective-permute-start.21
  110.6 1.7 constant_dynamic-update-slice_fusion.8
  112.3 7.6 %collective-permute-start.9 = (bf16[1152,384]{1,0:T(8,128)(2,1)S(1)}, bf16[1152,384]{1,0:T(8,128)(2,1)S(1)}, u32[]{:S(2)}, u32[]{:S(2)}) collective-permute-start(bf16[1152,384]{1,0:T(8,128)(2,1)S(1)} %bitcast.38), channel_id=1, source_target_pairs={{0,12},{1,13},{2,14},{3,15},{16,28},{17,29},{18,30},{19,31}} | collective-permute-start | bytes 2654216 | tf_op jit(solution)/shard_map/ppermute | solution.py:18
  119.9 1.3 constant_dynamic-update-slice_fusion.16
  121.3 1.5 collective-permute-start.10
  123.0 3.7 %collective-permute-start.11 = (bf16[1152,384]{1,0:T(8,128)(2,1)S(1)}, bf16[1152,384]{1,0:T(8,128)(2,1)S(1)}, u32[]{:S(2)}, u32[]{:S(2)}) collective-permute-start(bf16[1152,384]{1,0:T(8,128)(2,1)S(1)} %bitcast.40), channel_id=1, source_target_pairs={{0,4},{4,8},{8,12},{1,5},{5,9},{9,13},{2,6},{6,10},{10,14},{3,7},{... | collective-permute-start | bytes 2654216 | tf_op jit(solution)/shard_map/ppermute | solution.py:18
  126.7 1.3 constant_dynamic-update-slice_fusion.14
  128.2 12.9 %collective-permute-done.9 = bf16[1152,384]{1,0:T(8,128)(2,1)S(1)} collective-permute-done((bf16[1152,384]{1,0:T(8,128)(2,1)S(1)}, bf16[1152,384]{1,0:T(8,128)(2,1)S(1)}, u32[]{:S(2)}, u32[]{:S(2)}) %collective-permute-start.9) | collective-permute-done | bytes 884768 | tf_op jit(solution)/shard_map/ppermute | solution.py:18
  141.1 1.3 collective-permute-start.22
  142.4 1.0 constant_dynamic-update-slice_fusion.7
  143.4 16.6 %collective-permute-done.10 = bf16[1152,384]{1,0:T(8,128)(2,1)S(1)} collective-permute-done((bf16[1152,384]{1,0:T(8,128)(2,1)S(1)}, bf16[1152,384]{1,0:T(8,128)(2,1)S(1)}, u32[]{:S(2)}, u32[]{:S(2)}) %collective-permute-start.10) | collective-permute-done | bytes 884768 | tf_op jit(solution)/shard_map/ppermute | solution.py:18
  160.1 1.3 collective-permute-start.12
  162.4 14.6 %collective-permute-done.11 = bf16[1152,384]{1,0:T(8,128)(2,1)S(1)} collective-permute-done((bf16[1152,384]{1,0:T(8,128)(2,1)S(1)}, bf16[1152,384]{1,0:T(8,128)(2,1)S(1)}, u32[]{:S(2)}, u32[]{:S(2)}) %collective-permute-start.11) | collective-permute-done | bytes 884768 | tf_op jit(solution)/shard_map/ppermute | solution.py:18
  177.0 1.3 collective-permute-start.13
  178.2 1.0 constant_dynamic-update-slice_fusion.5
  180.3 1.3 collective-permute-start.14
  181.7 5.0 %collective-permute-done.21 = bf16[1152,384]{1,0:T(8,128)(2,1)S(1)} collective-permute-done((bf16[1152,384]{1,0:T(8,128)(2,1)S(1)}, bf16[1152,384]{1,0:T(8,128)(2,1)S(1)}, u32[]{:S(2)}, u32[]{:S(2)}) %collective-permute-start.21) | collective-permute-done | bytes 884768 | tf_op jit(solution)/shard_map/ppermute | solution.py:18
  188.5 15.1 %collective-permute-done.12 = bf16[1152,384]{1,0:T(8,128)(2,1)S(1)} collective-permute-done((bf16[1152,384]{1,0:T(8,128)(2,1)S(1)}, bf16[1152,384]{1,0:T(8,128)(2,1)S(1)}, u32[]{:S(2)}, u32[]{:S(2)}) %collective-permute-start.12) | collective-permute-done | bytes 884768 | tf_op jit(solution)/shard_map/ppermute | solution.py:18
  204.6 55.9 %collective-permute-done.13 = bf16[1152,384]{1,0:T(8,128)(2,1)S(1)} collective-permute-done((bf16[1152,384]{1,0:T(8,128)(2,1)S(1)}, bf16[1152,384]{1,0:T(8,128)(2,1)S(1)}, u32[]{:S(2)}, u32[]{:S(2)}) %collective-permute-start.13) | collective-permute-done | bytes 884768 | tf_op jit(solution)/shard_map/ppermute | solution.py:18
  260.5 1.0 constant_dynamic-update-slice_fusion.2
  261.7 1.1 constant_dynamic-update-slice_fusion.1
  262.7 2.0 copy-done
  265.5 22.9 %shard_map.55 = bf16[3,384,384]{2,1,0:T(8,128)(2,1)S(1)} custom-call(s32[3,8]{1,0:T(4,128)S(1)} %subtract_clamp_fusion.lists_ref, s32[23]{0:T(128)S(1)} %concatenate.9.counts_ref, bf16[3,384,384]{2,1,0:T(8,128)(2,1)S(1)} %bitcast.27, bf16[23,384,384]{2,1,0:T(8,128)(2,1)} %bitcast.5.refs_0_.refs_1_.refs_2_.refs_3_.refs_4_.refs_5_.refs_6_.refs_7_, ...), custom_call_target="tpu_custom_call" | custom-call | tf_op jit(solution)/shard_map/pallas_call | solution.py:73
  288.4 15.3 %all_to_all.73 = bf16[4,288,384]{2,1,0:T(8,128)(2,1)S(1)} all-to-all(bf16[4,288,384]{2,1,0:T(8,128)(2,1)S(1)} %bitcast.28), channel_id=1, replica_groups=mesh['clips'=2,'ctx'=4,'head'=4] {'head'}, dimensions={0} | all-to-all | bytes 1769472 | tf_op jit(solution)/shard_map/all_to_all | solution.py:114
  (57 shorter events, 12.1 us)
Async XLA Ops:
  0.0 22.7 %copy-start.4 = (s32[3]{0:T(128)S(1)}, s32[3]{0:T(128)}, u32[]{:S(2)}) copy-start(s32[3]{0:T(128)} %param.9) | copy-start | bytes 40
  0.0 30.7 %copy-start.1 = (bf16[288,1536]{1,0:T(8,128)(2,1)S(1)}, bf16[288,1536]{1,0:T(8,128)(2,1)}, u32[]{:S(2)}) copy-start(bf16[288,1536]{1,0:T(8,128)(2,1)} %param.5) | copy-start | bytes 2654212
  0.0 105.1 %copy-start.5 = (s32[3,8]{1,0:T(4,128)S(1)}, s32[3,8]{1,0:T(4,128)}, u32[]{:S(2)}) copy-start(s32[3,8]{1,0:T(4,128)} %param.8) | copy-start | bytes 292
  2.3 16.9 %all-to-all-start.2 = ((bf16[288,4,384]{2,0,1:T(8,128)(2,1)}), bf16[288,4,384]{2,0,1:T(8,128)(2,1)S(1)}, u32[]{:S(2)}, u32[]{:S(2)}) async-start(bf16[288,4,384]{2,0,1:T(8,128)(2,1)} %bitcast.24), calls=%async_computation.2 | async-start | bytes 1769472 | tf_op jit(solution)/shard_map/all_to_all | solution.py:85
  19.2 18.3 %all-to-all-start.1 = ((bf16[288,4,384]{2,0,1:T(8,128)(2,1)}), bf16[288,4,384]{2,0,1:T(8,128)(2,1)S(1)}, u32[]{:S(2)}, u32[]{:S(2)}) async-start(bf16[288,4,384]{2,0,1:T(8,128)(2,1)} %bitcast.25), calls=%async_computation.1 | async-start | bytes 1769472 | tf_op jit(solution)/shard_map/all_to_all | solution.py:84
  22.7 23.4 %collective-permute-start.1 = (s32[3]{0:T(128)S(1)}, s32[3]{0:T(128)S(1)}, u32[]{:S(2)}, u32[]{:S(2)}) collective-permute-start(s32[3]{0:T(128)S(1)} %copy-done.4), channel_id=1, source_target_pairs={{0,12},{1,13},{2,14},{3,15},{16,28},{17,29},{18,30},{19,31}} | collective-permute-start | bytes 44 | tf_op jit(solution)/shard_map/ppermute | solution.py:18
  29.5 12.4 %collective-permute-start = (s32[1]{0:T(128)}, s32[1]{0:T(128)}, u32[]{:S(2)}, u32[]{:S(2)}) collective-permute-start(s32[1]{0:T(128)} %get-tuple-element.10), channel_id=1, source_target_pairs={} | collective-permute-start | bytes 20 | tf_op jit(solution)/shard_map/ppermute | solution.py:18
  31.7 80.6 %collective-permute-start.17 = (bf16[1152,384]{1,0:T(8,128)(2,1)S(1)}, bf16[1152,384]{1,0:T(8,128)(2,1)}, u32[]{:S(2)}, u32[]{:S(2)}) collective-permute-start(bf16[1152,384]{1,0:T(8,128)(2,1)S(1)} %bitcast.45), channel_id=1, source_target_pairs={{0,12},{1,13},{2,14},{3,15},{16,28},{17,29},{18,30},{19,31}} | collective-permute-start | bytes 2654216 | tf_op jit(solution)/shard_map/ppermute | solution.py:18
  33.9 87.4 %collective-permute-start.18 = (bf16[1152,384]{1,0:T(8,128)(2,1)S(1)}, bf16[1152,384]{1,0:T(8,128)(2,1)S(1)}, u32[]{:S(2)}, u32[]{:S(2)}) collective-permute-start(bf16[1152,384]{1,0:T(8,128)(2,1)S(1)} %bitcast.46), channel_id=1, source_target_pairs={{0,8},{4,12},{1,9},{5,13},{2,10},{6,14},{3,11},{7,15},{16,24},{20,... | collective-permute-start | bytes 2654216 | tf_op jit(solution)/shard_map/ppermute | solution.py:18
  36.1 70.8 %collective-permute-start.16 = (bf16[384,384]{1,0:T(8,128)(2,1)}, bf16[384,384]{1,0:T(8,128)(2,1)}, u32[]{:S(2)}, u32[]{:S(2)}) collective-permute-start(bf16[384,384]{1,0:T(8,128)(2,1)} %get-tuple-element.6), channel_id=1, source_target_pairs={} | collective-permute-start | bytes 884744 | tf_op jit(solution)/shard_map/ppermute | solution.py:18
  37.5 228.0 %all-to-all-start = ((bf16[288,4,384]{2,0,1:T(8,128)(2,1)}), bf16[288,4,384]{2,0,1:T(8,128)(2,1)S(1)}, u32[]{:S(2)}, u32[]{:S(2)}) async-start(bf16[288,4,384]{2,0,1:T(8,128)(2,1)} %bitcast.26), calls=%async_computation | async-start | bytes 1769472 | tf_op jit(solution)/shard_map/all_to_all | solution.py:83
  41.9 1.2 collective-permute-start.7
  43.0 28.5 %collective-permute-start.2 = (s32[3]{0:T(128)S(1)}, s32[3]{0:T(128)S(1)}, u32[]{:S(2)}, u32[]{:S(2)}) collective-permute-start(s32[3]{0:T(128)S(1)} %copy-done.4), channel_id=1, source_target_pairs={{0,8},{4,12},{1,9},{5,13},{2,10},{6,14},{3,11},{7,15},{16,24},{20,... | collective-permute-start | bytes 44 | tf_op jit(solution)/shard_map/ppermute | solution.py:18
  46.1 26.7 %collective-permute-start.3 = (s32[3]{0:T(128)S(1)}, s32[3]{0:T(128)S(1)}, u32[]{:S(2)}, u32[]{:S(2)}) collective-permute-start(s32[3]{0:T(128)S(1)} %copy-done.4), channel_id=1, source_target_pairs={{0,4},{4,8},{8,12},{1,5},{5,9},{9,13},{2,6},{6,10},{10,14},{3,7},{... | collective-permute-start | bytes 44 | tf_op jit(solution)/shard_map/ppermute | solution.py:18
  71.5 31.6 %copy-start.6 = (s32[3]{0:T(128)}, s32[3]{0:T(128)S(1)}, u32[]{:S(2)}) copy-start(s32[3]{0:T(128)S(1)} %collective-permute-done.2) | copy-start | bytes 40
  71.5 23.9 %collective-permute-start.4 = (s32[3]{0:T(128)S(1)}, s32[3]{0:T(128)S(1)}, u32[]{:S(2)}, u32[]{:S(2)}) collective-permute-start(s32[3]{0:T(128)S(1)} %copy-done.4), channel_id=1, source_target_pairs={{4,0},{8,4},{12,8},{5,1},{9,5},{13,9},{6,2},{10,6},{14,10},{7,3},{... | collective-permute-start | bytes 44 | tf_op jit(solution)/shard_map/ppermute | solution.py:18
  72.8 30.3 %copy-start.7 = (s32[3]{0:T(128)}, s32[3]{0:T(128)S(1)}, u32[]{:S(2)}) copy-start(s32[3]{0:T(128)S(1)} %collective-permute-done.3) | copy-start | bytes 40
  72.8 25.3 %collective-permute-start.5 = (s32[3]{0:T(128)S(1)}, s32[3]{0:T(128)S(1)}, u32[]{:S(2)}, u32[]{:S(2)}) collective-permute-start(s32[3]{0:T(128)S(1)} %copy-done.4), channel_id=1, source_target_pairs={{8,0},{12,4},{9,1},{13,5},{10,2},{14,6},{11,3},{15,7},{24,16},{28,... | collective-permute-start | bytes 44 | tf_op jit(solution)/shard_map/ppermute | solution.py:18
  95.4 7.8 %copy-start.8 = (s32[3]{0:T(128)}, s32[3]{0:T(128)S(1)}, u32[]{:S(2)}) copy-start(s32[3]{0:T(128)S(1)} %collective-permute-done.4) | copy-start | bytes 40
  95.4 7.7 %collective-permute-start.6 = (s32[3]{0:T(128)S(1)}, s32[3]{0:T(128)S(1)}, u32[]{:S(2)}, u32[]{:S(2)}) collective-permute-start(s32[3]{0:T(128)S(1)} %copy-done.4), channel_id=1, source_target_pairs={{12,0},{13,1},{14,2},{15,3},{28,16},{29,17},{30,18},{31,19}} | collective-permute-start | bytes 44 | tf_op jit(solution)/shard_map/ppermute | solution.py:18
  98.2 5.0 %copy-start.9 = (s32[3]{0:T(128)}, s32[3]{0:T(128)S(1)}, u32[]{:S(2)}) copy-start(s32[3]{0:T(128)S(1)} %collective-permute-done.5) | copy-start | bytes 40
  98.2 24.8 %collective-permute-start.19 = (bf16[1152,384]{1,0:T(8,128)(2,1)S(1)}, bf16[1152,384]{1,0:T(8,128)(2,1)}, u32[]{:S(2)}, u32[]{:S(2)}) collective-permute-start(bf16[1152,384]{1,0:T(8,128)(2,1)S(1)} %bitcast.48), channel_id=1, source_target_pairs={{0,4},{4,8},{8,12},{1,5},{5,9},{9,13},{2,6},{6,10},{10,14},{3,7},{... | collective-permute-start | bytes 2654216 | tf_op jit(solution)/shard_map/ppermute | solution.py:18
  103.1 0.6 copy-start.10
  103.7 5.6 %collective-permute-start.8 = (bf16[384,384]{1,0:T(8,128)(2,1)}, bf16[384,384]{1,0:T(8,128)(2,1)}, u32[]{:S(2)}, u32[]{:S(2)}) collective-permute-start(bf16[384,384]{1,0:T(8,128)(2,1)} %get-tuple-element.8), channel_id=1, source_target_pairs={} | collective-permute-start | bytes 884744 | tf_op jit(solution)/shard_map/ppermute | solution.py:18
  107.0 73.3 %collective-permute-start.20 = (bf16[1152,384]{1,0:T(8,128)(2,1)S(1)}, bf16[1152,384]{1,0:T(8,128)(2,1)S(1)}, u32[]{:S(2)}, u32[]{:S(2)}) collective-permute-start(bf16[1152,384]{1,0:T(8,128)(2,1)S(1)} %bitcast.49), channel_id=1, source_target_pairs={{4,0},{8,4},{12,8},{5,1},{9,5},{13,9},{6,2},{10,6},{14,10},{7,3},{... | collective-permute-start | bytes 2654216 | tf_op jit(solution)/shard_map/ppermute | solution.py:18
  109.3 77.5 %collective-permute-start.21 = (bf16[1152,384]{1,0:T(8,128)(2,1)S(1)}, bf16[1152,384]{1,0:T(8,128)(2,1)S(1)}, u32[]{:S(2)}, u32[]{:S(2)}) collective-permute-start(bf16[1152,384]{1,0:T(8,128)(2,1)S(1)} %bitcast.50), channel_id=1, source_target_pairs={{8,0},{12,4},{9,1},{13,5},{10,2},{14,6},{11,3},{15,7},{24,16},{28,... | collective-permute-start | bytes 2654216 | tf_op jit(solution)/shard_map/ppermute | solution.py:18
  112.3 28.8 %collective-permute-start.9 = (bf16[1152,384]{1,0:T(8,128)(2,1)S(1)}, bf16[1152,384]{1,0:T(8,128)(2,1)S(1)}, u32[]{:S(2)}, u32[]{:S(2)}) collective-permute-start(bf16[1152,384]{1,0:T(8,128)(2,1)S(1)} %bitcast.38), channel_id=1, source_target_pairs={{0,12},{1,13},{2,14},{3,15},{16,28},{17,29},{18,30},{19,31}} | collective-permute-start | bytes 2654216 | tf_op jit(solution)/shard_map/ppermute | solution.py:18
  121.3 65.5 %copy-start.2 = (bf16[384,384]{1,0:T(8,128)(2,1)S(1)}, bf16[384,384]{1,0:T(8,128)(2,1)}, u32[]{:S(2)}) copy-start(bf16[384,384]{1,0:T(8,128)(2,1)} %get-tuple-element.5) | copy-start | bytes 884740
  121.3 38.8 %collective-permute-start.10 = (bf16[1152,384]{1,0:T(8,128)(2,1)S(1)}, bf16[1152,384]{1,0:T(8,128)(2,1)S(1)}, u32[]{:S(2)}, u32[]{:S(2)}) collective-permute-start(bf16[1152,384]{1,0:T(8,128)(2,1)S(1)} %bitcast.39), channel_id=1, source_target_pairs={{0,8},{4,12},{1,9},{5,13},{2,10},{6,14},{3,11},{7,15},{16,24},{20,... | collective-permute-start | bytes 2654216 | tf_op jit(solution)/shard_map/ppermute | solution.py:18
  122.9 64.7 %copy-start.3 = (bf16[384,384]{1,0:T(8,128)(2,1)S(1)}, bf16[384,384]{1,0:T(8,128)(2,1)}, u32[]{:S(2)}) copy-start(bf16[384,384]{1,0:T(8,128)(2,1)} %get-tuple-element.7) | copy-start | bytes 884740
  123.0 54.0 %collective-permute-start.11 = (bf16[1152,384]{1,0:T(8,128)(2,1)S(1)}, bf16[1152,384]{1,0:T(8,128)(2,1)S(1)}, u32[]{:S(2)}, u32[]{:S(2)}) collective-permute-start(bf16[1152,384]{1,0:T(8,128)(2,1)S(1)} %bitcast.40), channel_id=1, source_target_pairs={{0,4},{4,8},{8,12},{1,5},{5,9},{9,13},{2,6},{6,10},{10,14},{3,7},{... | collective-permute-start | bytes 2654216 | tf_op jit(solution)/shard_map/ppermute | solution.py:18
  141.1 46.5 %collective-permute-start.22 = (bf16[1152,384]{1,0:T(8,128)(2,1)S(1)}, bf16[1152,384]{1,0:T(8,128)(2,1)S(1)}, u32[]{:S(2)}, u32[]{:S(2)}) collective-permute-start(bf16[1152,384]{1,0:T(8,128)(2,1)S(1)} %bitcast.52), channel_id=1, source_target_pairs={{12,0},{13,1},{14,2},{15,3},{28,16},{29,17},{30,18},{31,19}} | collective-permute-start | bytes 2654216 | tf_op jit(solution)/shard_map/ppermute | solution.py:18
  160.1 43.5 %collective-permute-start.12 = (bf16[1152,384]{1,0:T(8,128)(2,1)S(1)}, bf16[1152,384]{1,0:T(8,128)(2,1)S(1)}, u32[]{:S(2)}, u32[]{:S(2)}) collective-permute-start(bf16[1152,384]{1,0:T(8,128)(2,1)S(1)} %bitcast.41), channel_id=1, source_target_pairs={{4,0},{8,4},{12,8},{5,1},{9,5},{13,9},{6,2},{10,6},{14,10},{7,3},{... | collective-permute-start | bytes 2654216 | tf_op jit(solution)/shard_map/ppermute | solution.py:18
  177.0 83.6 %collective-permute-start.13 = (bf16[1152,384]{1,0:T(8,128)(2,1)S(1)}, bf16[1152,384]{1,0:T(8,128)(2,1)S(1)}, u32[]{:S(2)}, u32[]{:S(2)}) collective-permute-start(bf16[1152,384]{1,0:T(8,128)(2,1)S(1)} %bitcast.42), channel_id=1, source_target_pairs={{8,0},{12,4},{9,1},{13,5},{10,2},{14,6},{11,3},{15,7},{24,16},{28,... | collective-permute-start | bytes 2654216 | tf_op jit(solution)/shard_map/ppermute | solution.py:18
  180.3 81.4 %collective-permute-start.14 = (bf16[1152,384]{1,0:T(8,128)(2,1)S(1)}, bf16[1152,384]{1,0:T(8,128)(2,1)S(1)}, u32[]{:S(2)}, u32[]{:S(2)}) collective-permute-start(bf16[1152,384]{1,0:T(8,128)(2,1)S(1)} %bitcast.44), channel_id=1, source_target_pairs={{12,0},{13,1},{14,2},{15,3},{28,16},{29,17},{30,18},{31,19}} | collective-permute-start | bytes 2654216 | tf_op jit(solution)/shard_map/ppermute | solution.py:18
  186.8 74.8 %collective-permute-start.23 = (bf16[384,384]{1,0:T(8,128)(2,1)S(1)}, bf16[384,384]{1,0:T(8,128)(2,1)S(1)}, u32[]{:S(2)}, u32[]{:S(2)}) collective-permute-start(bf16[384,384]{1,0:T(8,128)(2,1)S(1)} %copy-done.2), channel_id=1, source_target_pairs={} | collective-permute-start | bytes 884744 | tf_op jit(solution)/shard_map/ppermute | solution.py:18
  187.7 75.1 %collective-permute-start.15 = (bf16[384,384]{1,0:T(8,128)(2,1)S(1)}, bf16[384,384]{1,0:T(8,128)(2,1)S(1)}, u32[]{:S(2)}, u32[]{:S(2)}) collective-permute-start(bf16[384,384]{1,0:T(8,128)(2,1)S(1)} %copy-done.3), channel_id=1, source_target_pairs={} | collective-permute-start | bytes 884744 | tf_op jit(solution)/shard_map/ppermute | solution.py:18
  261.6 3.1 %copy-start = (bf16[8832,384]{1,0:T(8,128)(2,1)}, bf16[8832,384]{1,0:T(8,128)(2,1)S(1)}, u32[]{:S(2)}) copy-start(bf16[8832,384]{1,0:T(8,128)(2,1)S(1)} %constant_dynamic-update-slice_fusion.9) | copy-start | bytes 20348932

commit v2 on v1

v2 whole, which is shorter than its diff:
```python
import jax
import jax.numpy as jnp
from jax import lax
from jax.sharding import PartitionSpec as P
from jax.experimental import pallas as pl
from jax.experimental.pallas import tpu as pltpu

DH = 128
TILE = 384
NB = 8
REACH = 10
HOPS = 4


def shifted(array, axis, by):
    peers = lax.axis_size(axis)
    pairs = [(i, i + by) for i in range(peers) if 0 <= i + by < peers]
    return lax.ppermute(array, axis, pairs)


def attend_kernel(lists_ref, counts_ref, query_ref, *refs):
    key_refs = refs[:NB]
    value_refs = refs[NB : 2 * NB]
    out_ref = refs[2 * NB]
    tile = pl.program_id(0)
    query_rows = query_ref[...]
    slot_index = lax.broadcasted_iota(jnp.int32, (TILE, TILE), 1)
    scores = []
    for entry in range(NB):
        part = lax.dot_general(
            query_rows, key_refs[entry][...], (((1,), (1,)), ((), ())),
            preferred_element_type=jnp.float32,
        ) * DH ** (-0.5)
        live = slot_index < counts_ref[lists_ref[tile, entry]]
        scores.append(jnp.where(live, part, -jnp.inf))
    highest = scores[0].max(axis=1, keepdims=True)
    for part in scores[1:]:
        highest = jnp.maximum(highest, part.max(axis=1, keepdims=True))
    totals = jnp.zeros((TILE, 1), jnp.float32)
    summed = jnp.zeros((TILE, DH), jnp.float32)
    for entry in range(NB):
        weights = jnp.exp(scores[entry] - highest)
        totals = totals + weights.sum(axis=1, keepdims=True)
        summed = summed + jnp.dot(
            weights.astype(jnp.bfloat16), value_refs[entry][...],
            preferred_element_type=jnp.float32,
        )
    out_ref[...] = (summed / totals).astype(out_ref.dtype)


def attend(local_lists, ext_counts, query_tiles, ext_kv):
    tiles_here, _, local_width = query_tiles.shape
    local_heads = local_width // DH
    own = pl.BlockSpec((None, TILE, DH), lambda t, h, lists, counts: (t, 0, h))

    def listed(entry, offset):
        return pl.BlockSpec(
            (None, TILE, DH), lambda t, h, lists, counts: (lists[t, entry], 0, h + offset)
        )

    spec = pltpu.PrefetchScalarGridSpec(
        num_scalar_prefetch=2,
        grid=(tiles_here, local_heads),
        in_specs=[own] + [listed(e, 0) for e in range(NB)] + [listed(e, local_heads) for e in range(NB)],
        out_specs=own,
    )
    return pl.pallas_call(
        attend_kernel,
        grid_spec=spec,
        out_shape=jax.ShapeDtypeStruct(query_tiles.shape, query_tiles.dtype),
        compiler_params=pltpu.CompilerParams(vmem_limit_bytes=48 * 1024 * 1024),
    )(local_lists, ext_counts, query_tiles, *([ext_kv] * (2 * NB)))


def shards(queries, keys, values, neighbors, tile_counts):
    rows, width = queries.shape
    head_peers = lax.axis_size("head")
    group = width // head_peers
    stacked = jnp.stack([queries, keys, values], axis=1).reshape(rows, 3, head_peers, group)
    moved = lax.all_to_all(stacked, "head", split_axis=2, concat_axis=0, tiled=True)
    block_queries = moved[:, 0, 0]
    block_kv = moved[:, 1:, 0].reshape(rows * head_peers, 2 * group)
    tiles_here = tile_counts.shape[0]
    local_heads = group // DH
    ctx_peers = lax.axis_size("ctx")
    if ctx_peers <= 2 * HOPS + 1:
        ext_tiles = ctx_peers * tiles_here
        ext_kv = lax.all_gather(block_kv, "ctx", axis=0, tiled=True)
        ext_counts = lax.all_gather(tile_counts, "ctx", axis=0, tiled=True)
        first_tile = 0
    else:
        earlier = []
        later = []
        for distance in range(1, HOPS + 1):
            taken = min(tiles_here, REACH - (distance - 1) * tiles_here)
            rows_taken = taken * TILE
            earlier = [shifted((block_kv[-rows_taken:], tile_counts[-taken:]), "ctx", distance)] + earlier
            later = later + [shifted((block_kv[:rows_taken], tile_counts[:taken]), "ctx", -distance)]
        ext_tiles = tiles_here + 2 * REACH
        ext_kv = jnp.concatenate([p[0] for p in earlier] + [block_kv] + [p[0] for p in later], axis=0)
        ext_counts = jnp.concatenate([p[1] for p in earlier] + [tile_counts] + [p[1] for p in later], axis=0)
        first_tile = lax.axis_index("ctx") * tiles_here - REACH
    ext_kv = ext_kv.reshape(ext_tiles, TILE, 2 * group)
    local_lists = jnp.clip(neighbors - first_tile, 0, ext_tiles - 1).astype(jnp.int32)
    query_tiles = block_queries.reshape(tiles_here, TILE, group)
    outputs = attend(local_lists, ext_counts.astype(jnp.int32), query_tiles, ext_kv)
    outputs = outputs.reshape(tiles_here * TILE, group)
    return lax.all_to_all(outputs, "head", split_axis=0, concat_axis=1, tiled=True)


def solution(mesh):
    placed = (
        P(("clips", "ctx", "head"), None),
        P(("clips", "ctx", "head"), None),
        P(("clips", "ctx", "head"), None),
        P(("clips", "ctx"), None),
        P(("clips", "ctx")),
    )
    return jax.shard_map(
        shards,
        mesh=mesh,
        in_specs=placed,
        out_specs=P(("clips", "ctx", "head"), None),
        check_vma=False,
    )
```

time: 306 us -> 240 us (0.78)
  starting transfers between devices: 63.2 us -> 0.01 us
  waiting for transfers between devices: 175 us -> 119 us
  blocking collectives: 15.3 us -> 59.3 us
  between operations: 0.37 us -> 14.1 us
  local copies, waits for them, and re-layouts: 27.6 us -> 22 us
    ppermute x24 -> x0, waiting for transfers between devices: 165 us -> none  [shifted(): return lax.ppermute(array, axis, pairs)]
    all_gather x0 -> x1, waiting for transfers between devices: none -> 119 us  [shards(): ext_kv = lax.all_gather(block_kv, 'ctx', axis=0, tiled=True)]
    ppermute x24 -> x0, starting transfers between devices: 52 us -> none  [shifted(): return lax.ppermute(array, axis, pairs)]
    all_to_all x0 -> x1, blocking collectives: none -> 35.7 us  [shards(): lax.all_to_all(stacked, 'head', split_axis=2, concat_axis=0, tiled=True)]
    unnamed x38 -> x11, local copies, waits for them, and re-layouts: 16.1 us -> 0.84 us
    all_to_all x3 -> x0, starting transfers between devices: 11.2 us -> none  [the longest x1 4.24 us: shards(): lax.all_to_all(values, 'head', split_axis=1, concat_axis=0, tiled=True)]
    all_to_all x3 -> x0, waiting for transfers between devices: 10.5 us -> none  [the longest x1 10.5 us: shards(): lax.all_to_all(values, 'head', split_axis=1, concat_axis=0, tiled=True)]
    all_gather x0 -> x1, local copies, waits for them, and re-layouts: none -> 10.2 us  [shards(): ext_kv = lax.all_gather(block_kv, 'ctx', axis=0, tiled=True)]
  transfers between devices with their start and end apart: 27 -> 1, of which waited for: 10 -> 1; matrix products, arithmetic and copies ran while one was open for 7% -> 0% of each run, Pallas kernels for 0% -> 0%
where the time goes in v2:
time: 240 us; the launch traced here: 239 us
  waiting for transfers between devices  119 us (50%)
  blocking collectives  59.3 us (25%)
  Pallas kernels  22.9 us (10%)
  local copies, waits for them, and re-layouts  22 us (9%)
  between operations  14.1 us (6%)
    all_gather x1, waiting for transfers between devices, shards(): ext_kv = lax.all_gather(block_kv, 'ctx', axis=0, tiled=True)  119 us
    all_to_all x1, blocking collectives, shards(): lax.all_to_all(stacked, 'head', split_axis=2, concat_axis=0, tiled=True)  35.7 us
    pallas_call x1, Pallas kernels, attend(): pl.pallas_call(attend_kernel, grid_spec=spec, out_shape=jax.ShapeDtypeStr...  22.9 us
    all_to_all x1, blocking collectives, shards(): lax.all_to_all(outputs, 'head', split_axis=0, concat_axis=1, tiled=True)  15.2 us
    all_gather x1, local copies, waits for them, and re-layouts, shards(): ext_kv = lax.all_gather(block_kv, 'ctx', axis=0, tiled=True)  10.2 us
    unnamed x1, blocking collectives  8.44 us
    slice x2, local copies, waits for them, and re-layouts, shards(): block_kv = moved[:, 1:, 0].reshape(rows * head_peers, 2 * group)  5.3 us
  transfers between devices with their start and end apart: 1, of which 1 were waited for; matrix products, arithmetic and copies ran while one was open for 0% of the time, Pallas kernels for 0%

profile of v2, /device:TPU:0, one launch (start us, length us, event | category | flops | bytes accessed | tf_op | source)
XLA Modules:
  0.0 239.3 jit_solution(1282038841339364895)
XLA Ops:
  6.5 0.0 copy-start
  6.5 0.0 all-gather.2.cloned.1.call-start
  6.5 1.9 stack.12
  8.5 1.8 stack.13
  10.3 0.0 copy-done
  10.3 0.2 stack.14
  10.5 2.3 pad_maximum_fusion
  12.8 0.3 copy.14
  13.2 35.7 %all_to_all.37 = bf16[288,3,4,384]{3,0,1,2:T(8,128)(2,1)S(1)} all-to-all(bf16[288,3,4,384]{3,0,1,2:T(8,128)(2,1)S(1)} %copy.14), channel_id=1, replica_groups=mesh['clips'=2,'ctx'=4,'head'=4] {'head'}, dimensions={2} | all-to-all | bytes 5308416 | tf_op jit(solution)/shard_map/all_to_all | solution.py:80
  48.8 0.3 copy.15
  49.1 1.4 slice.9
  50.6 0.0 copy-start.3
  50.6 0.0 copy-start.2
  50.6 0.0 copy-start.1
  50.6 3.9 %copy.16 = bf16[1152,2,1,384]{0,3,1,2:T(8,128)(2,1)} copy(bf16[1152,2,1,384]{3,0,1,2:T(8,128)(2,1)} %slice.9) | data formatting | bytes 3538944 | tf_op jit(solution)/shard_map/slice | solution.py:82
  54.4 0.0 all-gather.2.cloned.1.call-update
  54.5 0.0 copy-done.3
  54.5 0.6 dynamic-slice
  55.7 0.0 copy-done.2
  55.7 0.2 dynamic-update-slice
  56.0 8.4 %all-reduce.counts_ref = s32[12]{0:T(128)S(1)} all-reduce(s32[12]{0:T(128)S(1)} %dynamic-update-slice), channel_id=1, replica_groups=mesh['clips'=2,'ctx'=4,'head'=4] {'ctx'}, use_global_device_ids=true, to_apply=%add | all-reduce | flops 12 | bytes 96
  64.4 0.0 copy-done.1
  64.4 0.1 slice.8
  64.5 118.6 %all-gather.2.cloned.1.call-done = bf16[4608,768]{0,1:T(8,128)(2,1)} async-done(((bf16[1152,768]{0,1:T(8,128)(2,1)}), bf16[4608,768]{0,1:T(8,128)(2,1)}) %all-gather.2.cloned.1.call-update) | async-done | bytes 7077904 | tf_op jit(solution)/shard_map/all_gather | solution.py:88
  183.1 10.2 %copy.17 = bf16[4608,768]{1,0:T(8,128)(2,1)} copy(bf16[4608,768]{0,1:T(8,128)(2,1)} %all-gather.2.cloned.1.call-done) | data formatting | bytes 14155776 | tf_op jit(solution)/shard_map/all_gather | solution.py:88
  193.3 22.9 %shard_map.55 = bf16[3,384,384]{2,1,0:T(8,128)(2,1)S(1)} custom-call(s32[3,8]{1,0:T(4,128)S(1)} %broadcast_clamp_fusion.lists_ref, s32[12]{0:T(128)S(1)} %all-reduce.counts_ref, bf16[3,384,384]{2,1,0:T(8,128)(2,1)S(1)} %bitcast.13, bf16[12,384,768]{2,1,0:T(8,128)(2,1)} %bitcast.15, bf16[12,384,768]{2,1,0:T(8,128)(2,1)} %bitcast.16, ...), custom_call_target="tpu_custom_call" | custom-call | tf_op jit(solution)/shard_map/pallas_call | solution.py:67
  216.3 15.2 %all_to_all.38 = bf16[4,288,384]{2,1,0:T(8,128)(2,1)S(1)} all-to-all(bf16[4,288,384]{2,1,0:T(8,128)(2,1)S(1)} %bitcast.14), channel_id=1, replica_groups=mesh['clips'=2,'ctx'=4,'head'=4] {'head'}, dimensions={0} | all-to-all | bytes 1769472 | tf_op jit(solution)/shard_map/all_to_all | solution.py:108
  231.5 1.0 copy.19
  (2 shorter events, 0.0 us)
Async XLA Ops:
  6.5 3.8 %copy-start = (bf16[288,1536]{1,0:T(8,128)(2,1)S(1)}, bf16[288,1536]{1,0:T(8,128)(2,1)}, u32[]{:S(2)}) copy-start(bf16[288,1536]{1,0:T(8,128)(2,1)} %param.7) | copy-start | bytes 2654212
  6.5 176.6 %all-gather.2.cloned.1.call-start = ((), (), s32[]{:S(2)}) async-start(), calls=%async_computation.2 | async-start | bytes 8847360 | tf_op jit(solution)/shard_map/all_gather | solution.py:88
  50.6 3.9 %copy-start.3 = (u32[32]{0:T(128)S(1)}, u32[32]{0:T(128)}, u32[]{:S(2)}) copy-start(u32[32]{0:T(128)} %constant.8) | copy-start | bytes 388
  50.6 5.2 %copy-start.2 = (s32[3]{0:T(128)S(1)}, s32[3]{0:T(128)}, u32[]{:S(2)}) copy-start(s32[3]{0:T(128)} %param.9) | copy-start | bytes 40
  50.6 13.9 %copy-start.1 = (s32[3,8]{1,0:T(4,128)S(1)}, s32[3,8]{1,0:T(4,128)}, u32[]{:S(2)}) copy-start(s32[3,8]{1,0:T(4,128)} %param.8) | copy-start | bytes 292
Sparse Core Ops, SparseCore 0:
  54.6 128.5 all-gather.1

commit v3 on v2

--- a/solution.py
+++ b/solution.py
@@ -76,10 +76,11 @@
     rows, width = queries.shape
     head_peers = lax.axis_size("head")
     group = width // head_peers
-    stacked = jnp.stack([queries, keys, values], axis=1).reshape(rows, 3, head_peers, group)
-    moved = lax.all_to_all(stacked, "head", split_axis=2, concat_axis=0, tiled=True)
-    block_queries = moved[:, 0, 0]
-    block_kv = moved[:, 1:, 0].reshape(rows * head_peers, 2 * group)
+    paired = jnp.concatenate(
+        [keys.reshape(rows, head_peers, group), values.reshape(rows, head_peers, group)], axis=2
+    )
+    block_kv = lax.all_to_all(paired, "head", split_axis=1, concat_axis=0, tiled=True)
+    block_kv = block_kv.reshape(rows * head_peers, 2 * group)
     tiles_here = tile_counts.shape[0]
     local_heads = group // DH
     ctx_peers = lax.axis_size("ctx")
@@ -102,6 +103,7 @@
         first_tile = lax.axis_index("ctx") * tiles_here - REACH
     ext_kv = ext_kv.reshape(ext_tiles, TILE, 2 * group)
     local_lists = jnp.clip(neighbors - first_tile, 0, ext_tiles - 1).astype(jnp.int32)
+    block_queries = lax.all_to_all(queries, "head", split_axis=1, concat_axis=0, tiled=True)
     query_tiles = block_queries.reshape(tiles_here, TILE, group)
     outputs = attend(local_lists, ext_counts.astype(jnp.int32), query_tiles, ext_kv)
     outputs = outputs.reshape(tiles_here * TILE, group)

time: 240 us -> 212 us (0.88)
  local copies, waits for them, and re-layouts: 22 us -> 6.34 us
  waiting for transfers between devices: 119 us -> 110 us
  blocking collectives: 59.3 us -> 53.8 us
  starting transfers between devices: 0.01 us -> 3.51 us
    all_gather x1 -> x0, local copies, waits for them, and re-layouts: 10.2 us -> none  [shards(): ext_kv = lax.all_gather(block_kv, 'ctx', axis=0, tiled=True)]
    all_to_all x1, blocking collectives: 35.7 us -> 26.3 us  [shards(): lax.all_to_all(paired, 'head', split_axis=1, concat_axis=0, tiled=True)]
    all_gather x1, waiting for transfers between devices: 119 us -> 110 us  [shards(): ext_kv = lax.all_gather(block_kv, 'ctx', axis=0, tiled=True)]
    slice x3 -> x0, local copies, waits for them, and re-layouts: 5.39 us -> none  [the longest x2 5.3 us: shards(): block_kv = moved[:, 1:, 0].reshape(rows * head_peers, 2 * group)]
    another operation x4 -> x0, local copies, waits for them, and re-layouts: 4.29 us -> none  [shards(): jnp.stack([queries, keys, values], axis=1)]
    unnamed x1, blocking collectives: 8.44 us -> 12.3 us
    all_to_all x0 -> x1, starting transfers between devices: none -> 3.5 us  [shards(): lax.all_to_all(queries, 'head', split_axis=1, concat_axis=0, tiled=True)]
  transfers between devices with their start and end apart: 1 -> 2, of which waited for: 1 -> 1; matrix products, arithmetic and copies ran while one was open for 0% -> 1% of each run, Pallas kernels for 0% -> 0%
where the time goes in v3:
time: 212 us; the launch traced here: 211 us
  waiting for transfers between devices  110 us (52%)
  blocking collectives  53.8 us (25%)
  Pallas kernels  22.9 us (11%)
  between operations  14.1 us (7%)
  local copies, waits for them, and re-layouts  6.34 us (3%)
  starting transfers between devices  3.51 us (2%)
    all_gather x1, waiting for transfers between devices, shards(): ext_kv = lax.all_gather(block_kv, 'ctx', axis=0, tiled=True)  110 us
    all_to_all x1, blocking collectives, shards(): lax.all_to_all(paired, 'head', split_axis=1, concat_axis=0, tiled=True)  26.3 us
    pallas_call x1, Pallas kernels, attend(): pl.pallas_call(attend_kernel, grid_spec=spec, out_shape=jax.ShapeDtypeStr...  22.9 us
    all_to_all x1, blocking collectives, shards(): lax.all_to_all(outputs, 'head', split_axis=0, concat_axis=1, tiled=True)  15.2 us
    unnamed x1, blocking collectives  12.3 us
  transfers between devices with their start and end apart: 2, of which 1 were waited for; matrix products, arithmetic and copies ran while one was open for 1% of the time, Pallas kernels for 0%

profile of v3, /device:TPU:0, one launch (start us, length us, event | category | flops | bytes accessed | tf_op | source)
XLA Modules:
  0.0 211.4 jit_solution(4339548432249398738)
XLA Ops:
  6.5 0.0 copy-start
  6.5 0.0 all-gather.2.cloned.1.call-start
  6.5 1.9 reshape.26
  8.5 0.0 copy-done
  8.5 0.2 reshape.27
  8.7 0.8 pad_maximum_fusion
  9.4 0.2 copy.12
  9.7 26.3 %all_to_all.50 = bf16[288,4,768]{2,0,1:T(8,128)(2,1)} all-to-all(bf16[288,4,768]{2,0,1:T(8,128)(2,1)S(1)} %copy.12), channel_id=1, replica_groups=mesh['clips'=2,'ctx'=4,'head'=4] {'head'}, dimensions={1} | all-to-all | bytes 3538944 | tf_op jit(solution)/shard_map/all_to_all | solution.py:82
  36.0 0.0 copy-start.1
  36.0 0.0 all-gather.2.cloned.1.call-update
  36.0 1.1 copy-done.1
  37.1 0.0 copy-start.4
  37.1 0.0 copy-start.3
  37.1 0.0 copy-start.2
  37.1 1.0 copy.17
  38.1 3.5 %all-to-all-start = ((bf16[288,4,384]{2,0,1:T(8,128)(2,1)}), bf16[288,4,384]{2,0,1:T(8,128)(2,1)S(1)}, u32[]{:S(2)}, u32[]{:S(2)}) async-start(bf16[288,4,384]{2,0,1:T(8,128)(2,1)} %bitcast.17), calls=%async_computation | async-start | bytes 1769472 | tf_op jit(solution)/shard_map/all_to_all | solution.py:106
  41.7 0.0 copy-done.4
  41.7 0.6 dynamic-slice
  42.9 0.0 copy-done.3
  42.9 0.2 dynamic-update-slice
  43.2 12.3 %all-reduce.counts_ref = s32[12]{0:T(128)S(1)} all-reduce(s32[12]{0:T(128)S(1)} %dynamic-update-slice), channel_id=1, replica_groups=mesh['clips'=2,'ctx'=4,'head'=4] {'ctx'}, use_global_device_ids=true, to_apply=%add | all-reduce | flops 12 | bytes 96
  55.5 0.0 copy-done.2
  55.5 0.0 all-to-all-done
  55.5 109.9 %all-gather.2.cloned.1.call-done = bf16[4608,768]{1,0:T(8,128)(2,1)} async-done(((bf16[1152,768]{1,0:T(8,128)(2,1)}), bf16[4608,768]{1,0:T(8,128)(2,1)}) %all-gather.2.cloned.1.call-update) | async-done | bytes 7077904 | tf_op jit(solution)/shard_map/all_gather | solution.py:89
  165.4 22.9 %shard_map.55 = bf16[3,384,384]{2,1,0:T(8,128)(2,1)S(1)} custom-call(s32[3,8]{1,0:T(4,128)S(1)} %broadcast_clamp_fusion.lists_ref, s32[12]{0:T(128)S(1)} %all-reduce.counts_ref, bf16[3,384,384]{2,1,0:T(8,128)(2,1)S(1)} %bitcast.18, bf16[12,384,768]{2,1,0:T(8,128)(2,1)} %bitcast.20, bf16[12,384,768]{2,1,0:T(8,128)(2,1)} %bitcast.21, ...), custom_call_target="tpu_custom_call" | custom-call | tf_op jit(solution)/shard_map/pallas_call | solution.py:67
  188.3 15.2 %all_to_all.51 = bf16[4,288,384]{2,1,0:T(8,128)(2,1)S(1)} all-to-all(bf16[4,288,384]{2,1,0:T(8,128)(2,1)S(1)} %bitcast.19), channel_id=1, replica_groups=mesh['clips'=2,'ctx'=4,'head'=4] {'head'}, dimensions={0} | all-to-all | bytes 1769472 | tf_op jit(solution)/shard_map/all_to_all | solution.py:110
  203.5 1.0 copy.15
  (2 shorter events, 0.0 us)
Async XLA Ops:
  6.5 1.9 copy-start
  6.5 158.8 %all-gather.2.cloned.1.call-start = ((), (), s32[]{:S(2)}) async-start(), calls=%async_computation.3 | async-start | bytes 8847360 | tf_op jit(solution)/shard_map/all_gather | solution.py:89
  36.0 1.2 copy-start.1
  37.1 4.5 %copy-start.4 = (u32[32]{0:T(128)S(1)}, u32[32]{0:T(128)}, u32[]{:S(2)}) copy-start(u32[32]{0:T(128)} %constant.8) | copy-start | bytes 388
  37.1 5.8 %copy-start.3 = (s32[3]{0:T(128)S(1)}, s32[3]{0:T(128)}, u32[]{:S(2)}) copy-start(s32[3]{0:T(128)} %param.9) | copy-start | bytes 40
  37.1 18.3 %copy-start.2 = (s32[3,8]{1,0:T(4,128)S(1)}, s32[3,8]{1,0:T(4,128)}, u32[]{:S(2)}) copy-start(s32[3,8]{1,0:T(4,128)} %param.8) | copy-start | bytes 292
  38.1 17.3 %all-to-all-start = ((bf16[288,4,384]{2,0,1:T(8,128)(2,1)}), bf16[288,4,384]{2,0,1:T(8,128)(2,1)S(1)}, u32[]{:S(2)}, u32[]{:S(2)}) async-start(bf16[288,4,384]{2,0,1:T(8,128)(2,1)} %bitcast.17), calls=%async_computation | async-start | bytes 1769472 | tf_op jit(solution)/shard_map/all_to_all | solution.py:106
Sparse Core Ops, SparseCore 0:
  36.1 129.1 all-gather.1

commit v4 on v3

--- a/solution.py
+++ b/solution.py
@@ -48,26 +48,28 @@
     out_ref[...] = (summed / totals).astype(out_ref.dtype)
 
 
-def attend(local_lists, ext_counts, query_tiles, ext_kv):
+def attend(local_lists, ext_counts, query_tiles, ext_kv, head):
     tiles_here, _, local_width = query_tiles.shape
     local_heads = local_width // DH
-    own = pl.BlockSpec((None, TILE, DH), lambda t, h, lists, counts: (t, 0, h))
+    own = pl.BlockSpec((None, TILE, DH), lambda t, h, lists, counts: (t, 0, h + head))
+    back = pl.BlockSpec((None, TILE, DH), lambda t, h, lists, counts: (t, 0, 0))
 
     def listed(entry, offset):
         return pl.BlockSpec(
-            (None, TILE, DH), lambda t, h, lists, counts: (lists[t, entry], 0, h + offset)
+            (None, TILE, DH),
+            lambda t, h, lists, counts: (lists[t, entry], 0, h + head + offset),
         )
 
     spec = pltpu.PrefetchScalarGridSpec(
         num_scalar_prefetch=2,
-        grid=(tiles_here, local_heads),
+        grid=(tiles_here, 1),
         in_specs=[own] + [listed(e, 0) for e in range(NB)] + [listed(e, local_heads) for e in range(NB)],
-        out_specs=own,
+        out_specs=back,
     )
     return pl.pallas_call(
         attend_kernel,
         grid_spec=spec,
-        out_shape=jax.ShapeDtypeStruct(query_tiles.shape, query_tiles.dtype),
+        out_shape=jax.ShapeDtypeStruct((tiles_here, TILE, DH), query_tiles.dtype),
         compiler_params=pltpu.CompilerParams(vmem_limit_bytes=48 * 1024 * 1024),
     )(local_lists, ext_counts, query_tiles, *([ext_kv] * (2 * NB)))
 
@@ -105,9 +107,13 @@
     local_lists = jnp.clip(neighbors - first_tile, 0, ext_tiles - 1).astype(jnp.int32)
     block_queries = lax.all_to_all(queries, "head", split_axis=1, concat_axis=0, tiled=True)
     query_tiles = block_queries.reshape(tiles_here, TILE, group)
-    outputs = attend(local_lists, ext_counts.astype(jnp.int32), query_tiles, ext_kv)
-    outputs = outputs.reshape(tiles_here * TILE, group)
-    return lax.all_to_all(outputs, "head", split_axis=0, concat_axis=1, tiled=True)
+    returned = []
+    for head in range(local_heads):
+        outputs = attend(local_lists, ext_counts.astype(jnp.int32), query_tiles, ext_kv, head)
+        outputs = outputs.reshape(tiles_here * TILE, DH)
+        returned.append(lax.all_to_all(outputs, "head", split_axis=0, concat_axis=1, tiled=True))
+    joined = jnp.stack([piece.reshape(rows, head_peers, DH) for piece in returned], axis=2)
+    return joined.reshape(rows, width)
 
 
 def solution(mesh):

time: 212 us -> 220 us (1.038)
  starting transfers between devices: 3.51 us -> 10.4 us
  blocking collectives: 53.8 us -> 47.9 us
  Pallas kernels: 22.9 us -> 27.7 us
    all_to_all x0 -> x2, starting transfers between devices: none -> 6.93 us  [shards(): lax.all_to_all(outputs, 'head', split_axis=0, concat_axis=1, tiled=True)]
    all_to_all x1, blocking collectives: 15.2 us -> 9.39 us  [shards(): lax.all_to_all(outputs, 'head', split_axis=0, concat_axis=1, tiled=True)]
    pallas_call x1 -> x3, Pallas kernels: 22.9 us -> 27.7 us  [attend(): pl.pallas_call(attend_kernel, grid_spec=spec, out_shape=jax.ShapeDtypeStr...]
  transfers between devices with their start and end apart: 2 -> 4, of which waited for: 1 -> 1; matrix products, arithmetic and copies ran while one was open for 1% -> 1% of each run, Pallas kernels for 0% -> 8%
where the time goes in v4:
time: 220 us; the launch traced here: 219 us
  waiting for transfers between devices  110 us (50%)
  blocking collectives  47.9 us (22%)
  Pallas kernels  27.7 us (13%)
  between operations  14.2 us (6%)
  starting transfers between devices  10.4 us (5%)
  local copies, waits for them, and re-layouts  7.96 us (4%)
    all_gather x1, waiting for transfers between devices, shards(): ext_kv = lax.all_gather(block_kv, 'ctx', axis=0, tiled=True)  110 us
    pallas_call x3, Pallas kernels, attend(): pl.pallas_call(attend_kernel, grid_spec=spec, out_shape=jax.ShapeDtypeStr...  27.7 us
    all_to_all x1, blocking collectives, shards(): lax.all_to_all(paired, 'head', split_axis=1, concat_axis=0, tiled=True)  26.3 us
    unnamed x1, blocking collectives  12.2 us
    all_to_all x1, blocking collectives, shards(): lax.all_to_all(outputs, 'head', split_axis=0, concat_axis=1, tiled=True)  9.39 us
    all_to_all x2, starting transfers between devices, shards(): lax.all_to_all(outputs, 'head', split_axis=0, concat_axis=1, tiled=True)  6.93 us
  transfers between devices with their start and end apart: 4, of which 1 were waited for; matrix products, arithmetic and copies ran while one was open for 1% of the time, Pallas kernels for 8%

profile of v4, /device:TPU:0, one launch (start us, length us, event | category | flops | bytes accessed | tf_op | source)
XLA Modules:
  0.0 218.9 jit_solution(2556913910589489662)
XLA Ops:
  6.5 0.0 copy-start
  6.5 0.0 all-gather.2.cloned.1.call-start
  6.5 1.9 reshape.42
  8.5 0.0 copy-done
  8.5 0.2 reshape.43
  8.7 0.8 pad_maximum_fusion
  9.4 0.2 copy.20
  9.7 26.3 %all_to_all.79 = bf16[288,4,768]{2,0,1:T(8,128)(2,1)} all-to-all(bf16[288,4,768]{2,0,1:T(8,128)(2,1)S(1)} %copy.20), channel_id=1, replica_groups=mesh['clips'=2,'ctx'=4,'head'=4] {'head'}, dimensions={1} | all-to-all | bytes 3538944 | tf_op jit(solution)/shard_map/all_to_all | solution.py:84
  36.0 0.0 copy-start.1
  36.0 0.0 all-gather.2.cloned.1.call-update
  36.0 1.1 copy-done.1
  37.1 0.0 copy-start.4
  37.1 0.0 copy-start.3
  37.1 0.0 copy-start.2
  37.1 1.0 copy.24
  38.1 3.5 %all-to-all-start = ((bf16[288,4,384]{2,0,1:T(8,128)(2,1)}), bf16[288,4,384]{2,0,1:T(8,128)(2,1)S(1)}, u32[]{:S(2)}, u32[]{:S(2)}) async-start(bf16[288,4,384]{2,0,1:T(8,128)(2,1)} %bitcast.25), calls=%async_computation | async-start | bytes 1769472 | tf_op jit(solution)/shard_map/all_to_all | solution.py:108
  41.7 0.0 copy-done.4
  41.7 0.7 dynamic-slice
  43.0 0.0 copy-done.3
  43.0 0.2 dynamic-update-slice
  43.3 12.2 %all-reduce.counts_ref = s32[12]{0:T(128)S(1)} all-reduce(s32[12]{0:T(128)S(1)} %dynamic-update-slice), channel_id=1, replica_groups=mesh['clips'=2,'ctx'=4,'head'=4] {'ctx'}, use_global_device_ids=true, to_apply=%add | all-reduce | flops 12 | bytes 96
  55.5 0.0 copy-done.2
  55.5 0.0 all-to-all-done
  55.5 109.8 %all-gather.2.cloned.1.call-done = bf16[4608,768]{1,0:T(8,128)(2,1)} async-done(((bf16[1152,768]{1,0:T(8,128)(2,1)}), bf16[4608,768]{1,0:T(8,128)(2,1)}) %all-gather.2.cloned.1.call-update) | async-done | bytes 7077904 | tf_op jit(solution)/shard_map/all_gather | solution.py:91
  165.4 9.4 %shard_map.56 = bf16[3,384,128]{2,1,0:T(8,128)(2,1)} custom-call(s32[3,8]{1,0:T(4,128)S(1)} %broadcast_clamp_fusion.lists_ref, s32[12]{0:T(128)S(1)} %all-reduce.counts_ref, bf16[3,384,384]{2,1,0:T(8,128)(2,1)S(1)} %bitcast.26, bf16[12,384,768]{2,1,0:T(8,128)(2,1)} %bitcast.30, bf16[12,384,768]{2,1,0:T(8,128)(2,1)} %bitcast.31, ...), custom_call_target="tpu_custom_call" | custom-call | tf_op jit(solution)/shard_map/pallas_call | solution.py:69
  174.7 3.5 %all-to-all-start.3 = ((bf16[4,288,128]{2,1,0:T(8,128)(2,1)}), bf16[4,288,128]{2,1,0:T(8,128)(2,1)S(1)}, u32[]{:S(2)}, u32[]{:S(2)}) async-start(bf16[4,288,128]{2,1,0:T(8,128)(2,1)} %bitcast.11), calls=%async_computation.3 | async-start | bytes 589824 | tf_op jit(solution)/shard_map/all_to_all | solution.py:114
  178.2 9.4 %shard_map.57 = bf16[3,384,128]{2,1,0:T(8,128)(2,1)} custom-call(s32[3,8]{1,0:T(4,128)S(1)} %broadcast_clamp_fusion.lists_ref, s32[12]{0:T(128)S(1)} %all-reduce.counts_ref, bf16[3,384,384]{2,1,0:T(8,128)(2,1)S(1)} %bitcast.27, bf16[12,384,768]{2,1,0:T(8,128)(2,1)} %bitcast.53, bf16[12,384,768]{2,1,0:T(8,128)(2,1)} %bitcast.47, ...), custom_call_target="tpu_custom_call" | custom-call | tf_op jit(solution)/shard_map/pallas_call | solution.py:69
  187.6 0.0 all-to-all-done.3
  187.6 3.5 %all-to-all-start.4 = ((bf16[4,288,128]{2,1,0:T(8,128)(2,1)}), bf16[4,288,128]{2,1,0:T(8,128)(2,1)S(1)}, u32[]{:S(2)}, u32[]{:S(2)}) async-start(bf16[4,288,128]{2,1,0:T(8,128)(2,1)} %bitcast.14), calls=%async_computation.4 | async-start | bytes 589824 | tf_op jit(solution)/shard_map/all_to_all | solution.py:114
  191.1 8.9 %shard_map.55 = bf16[3,384,128]{2,1,0:T(8,128)(2,1)S(1)} custom-call(s32[3,8]{1,0:T(4,128)S(1)} %broadcast_clamp_fusion.lists_ref, s32[12]{0:T(128)S(1)} %all-reduce.counts_ref, bf16[3,384,384]{2,1,0:T(8,128)(2,1)S(1)} %bitcast.28, bf16[12,384,768]{2,1,0:T(8,128)(2,1)} %bitcast.62, bf16[12,384,768]{2,1,0:T(8,128)(2,1)} %bitcast.63, ...), custom_call_target="tpu_custom_call" | custom-call | tf_op jit(solution)/shard_map/pallas_call | solution.py:69
  200.0 0.0 all-to-all-done.4
  200.0 9.4 %all_to_all.80 = bf16[4,288,128]{2,1,0:T(8,128)(2,1)S(1)} all-to-all(bf16[4,288,128]{2,1,0:T(8,128)(2,1)S(1)} %bitcast.29), channel_id=1, replica_groups=mesh['clips'=2,'ctx'=4,'head'=4] {'head'}, dimensions={0} | all-to-all | bytes 589824 | tf_op jit(solution)/shard_map/all_to_all | solution.py:114
  209.4 0.1 pad_maximum_fusion.1
  209.5 0.6 copy.21
  210.1 2.0 reshape.46
  (2 shorter events, 0.0 us)
Async XLA Ops:
  6.5 1.9 copy-start
  6.5 158.8 %all-gather.2.cloned.1.call-start = ((), (), s32[]{:S(2)}) async-start(), calls=%async_computation.5 | async-start | bytes 8847360 | tf_op jit(solution)/shard_map/all_gather | solution.py:91
  36.0 1.2 copy-start.1
  37.1 4.5 %copy-start.4 = (u32[32]{0:T(128)S(1)}, u32[32]{0:T(128)}, u32[]{:S(2)}) copy-start(u32[32]{0:T(128)} %constant.8) | copy-start | bytes 388
  37.1 5.9 %copy-start.3 = (s32[3]{0:T(128)S(1)}, s32[3]{0:T(128)}, u32[]{:S(2)}) copy-start(s32[3]{0:T(128)} %param.9) | copy-start | bytes 40
  37.1 18.4 %copy-start.2 = (s32[3,8]{1,0:T(4,128)S(1)}, s32[3,8]{1,0:T(4,128)}, u32[]{:S(2)}) copy-start(s32[3,8]{1,0:T(4,128)} %param.8) | copy-start | bytes 292
  38.1 17.4 %all-to-all-start = ((bf16[288,4,384]{2,0,1:T(8,128)(2,1)}), bf16[288,4,384]{2,0,1:T(8,128)(2,1)S(1)}, u32[]{:S(2)}, u32[]{:S(2)}) async-start(bf16[288,4,384]{2,0,1:T(8,128)(2,1)} %bitcast.25), calls=%async_computation | async-start | bytes 1769472 | tf_op jit(solution)/shard_map/all_to_all | solution.py:108
  174.7 12.9 %all-to-all-start.3 = ((bf16[4,288,128]{2,1,0:T(8,128)(2,1)}), bf16[4,288,128]{2,1,0:T(8,128)(2,1)S(1)}, u32[]{:S(2)}, u32[]{:S(2)}) async-start(bf16[4,288,128]{2,1,0:T(8,128)(2,1)} %bitcast.11), calls=%async_computation.3 | async-start | bytes 589824 | tf_op jit(solution)/shard_map/all_to_all | solution.py:114
  187.6 12.4 %all-to-all-start.4 = ((bf16[4,288,128]{2,1,0:T(8,128)(2,1)}), bf16[4,288,128]{2,1,0:T(8,128)(2,1)S(1)}, u32[]{:S(2)}, u32[]{:S(2)}) async-start(bf16[4,288,128]{2,1,0:T(8,128)(2,1)} %bitcast.14), calls=%async_computation.4 | async-start | bytes 589824 | tf_op jit(solution)/shard_map/all_to_all | solution.py:114
Sparse Core Ops, SparseCore 0:
  36.1 129.2 all-gather.1

commit v5 on v3

--- a/solution.py
+++ b/solution.py
@@ -48,7 +48,7 @@
     out_ref[...] = (summed / totals).astype(out_ref.dtype)
 
 
-def attend(local_lists, ext_counts, query_tiles, ext_kv):
+def attend(local_lists, ext_counts, query_tiles, ext_keys, ext_values):
     tiles_here, _, local_width = query_tiles.shape
     local_heads = local_width // DH
     own = pl.BlockSpec((None, TILE, DH), lambda t, h, lists, counts: (t, 0, h))
@@ -61,7 +61,7 @@
     spec = pltpu.PrefetchScalarGridSpec(
         num_scalar_prefetch=2,
         grid=(tiles_here, local_heads),
-        in_specs=[own] + [listed(e, 0) for e in range(NB)] + [listed(e, local_heads) for e in range(NB)],
+        in_specs=[own] + [listed(e, 0) for e in range(NB)] * 2,
         out_specs=own,
     )
     return pl.pallas_call(
@@ -69,27 +69,27 @@
         grid_spec=spec,
         out_shape=jax.ShapeDtypeStruct(query_tiles.shape, query_tiles.dtype),
         compiler_params=pltpu.CompilerParams(vmem_limit_bytes=48 * 1024 * 1024),
-    )(local_lists, ext_counts, query_tiles, *([ext_kv] * (2 * NB)))
+    )(local_lists, ext_counts, query_tiles, *([ext_keys] * NB), *([ext_values] * NB))
 
 
 def shards(queries, keys, values, neighbors, tile_counts):
     rows, width = queries.shape
     head_peers = lax.axis_size("head")
     group = width // head_peers
-    paired = jnp.concatenate(
-        [keys.reshape(rows, head_peers, group), values.reshape(rows, head_peers, group)], axis=2
-    )
-    block_kv = lax.all_to_all(paired, "head", split_axis=1, concat_axis=0, tiled=True)
-    block_kv = block_kv.reshape(rows * head_peers, 2 * group)
+    block_keys = lax.all_to_all(keys, "head", split_axis=1, concat_axis=0, tiled=True)
     tiles_here = tile_counts.shape[0]
     local_heads = group // DH
     ctx_peers = lax.axis_size("ctx")
     if ctx_peers <= 2 * HOPS + 1:
         ext_tiles = ctx_peers * tiles_here
-        ext_kv = lax.all_gather(block_kv, "ctx", axis=0, tiled=True)
+        ext_keys = lax.all_gather(block_keys, "ctx", axis=0, tiled=True)
+        block_values = lax.all_to_all(values, "head", split_axis=1, concat_axis=0, tiled=True)
+        ext_values = lax.all_gather(block_values, "ctx", axis=0, tiled=True)
         ext_counts = lax.all_gather(tile_counts, "ctx", axis=0, tiled=True)
         first_tile = 0
     else:
+        block_values = lax.all_to_all(values, "head", split_axis=1, concat_axis=0, tiled=True)
+        block_kv = jnp.concatenate([block_keys, block_values], axis=1)
         earlier = []
         later = []
         for distance in range(1, HOPS + 1):
@@ -99,13 +99,16 @@
             later = later + [shifted((block_kv[:rows_taken], tile_counts[:taken]), "ctx", -distance)]
         ext_tiles = tiles_here + 2 * REACH
         ext_kv = jnp.concatenate([p[0] for p in earlier] + [block_kv] + [p[0] for p in later], axis=0)
+        ext_keys = ext_kv[:, :group]
+        ext_values = ext_kv[:, group:]
         ext_counts = jnp.concatenate([p[1] for p in earlier] + [tile_counts] + [p[1] for p in later], axis=0)
         first_tile = lax.axis_index("ctx") * tiles_here - REACH
-    ext_kv = ext_kv.reshape(ext_tiles, TILE, 2 * group)
+    ext_keys = ext_keys.reshape(ext_tiles, TILE, group)
+    ext_values = ext_values.reshape(ext_tiles, TILE, group)
     local_lists = jnp.clip(neighbors - first_tile, 0, ext_tiles - 1).astype(jnp.int32)
     block_queries = lax.all_to_all(queries, "head", split_axis=1, concat_axis=0, tiled=True)
     query_tiles = block_queries.reshape(tiles_here, TILE, group)
-    outputs = attend(local_lists, ext_counts.astype(jnp.int32), query_tiles, ext_kv)
+    outputs = attend(local_lists, ext_counts.astype(jnp.int32), query_tiles, ext_keys, ext_values)
     outputs = outputs.reshape(tiles_here * TILE, group)
     return lax.all_to_all(outputs, "head", split_axis=0, concat_axis=1, tiled=True)
 

time: 212 us -> 215 us (1.014)
  blocking collectives: 53.8 us -> 57.6 us
    all_to_all x1 -> x2, blocking collectives: 26.3 us -> 32.9 us  [the longest x1 16.9 us: shards(): lax.all_to_all(keys, 'head', split_axis=1, concat_axis=0, tiled=True)]
    unnamed x1, blocking collectives: 12.3 us -> 9.44 us
    all_gather x1 -> x2, waiting for transfers between devices: 110 us -> 108 us  [the longest x1 70.1 us: shards(): ext_values = lax.all_gather(block_values, 'ctx', axis=0, tiled=True)]
  transfers between devices with their start and end apart: 2 -> 3, of which waited for: 1 -> 3; matrix products, arithmetic and copies ran while one was open for 1% -> 1% of each run, Pallas kernels for 0% -> 0%
where the time goes in v5:
time: 215 us
  waiting for transfers between devices  109 us (51%)
  blocking collectives  57.6 us (27%)
  Pallas kernels  23.6 us (11%)
  between operations  14.2 us (7%)
  local copies, waits for them, and re-layouts  6.36 us (3%)
  starting transfers between devices  3.55 us (2%)
    all_gather x1, waiting for transfers between devices, shards(): ext_values = lax.all_gather(block_values, 'ctx', axis=0, tiled=True)  70.1 us
    all_gather x1, waiting for transfers between devices, shards(): ext_keys = lax.all_gather(block_keys, 'ctx', axis=0, tiled=True)  37.7 us
    pallas_call x1, Pallas kernels, attend(): pl.pallas_call(attend_kernel, grid_spec=spec, out_shape=jax.ShapeDtypeStr...  23.6 us
    all_to_all x1, blocking collectives, shards(): lax.all_to_all(keys, 'head', split_axis=1, concat_axis=0, tiled=True)  16.9 us
    all_to_all x1, blocking collectives, shards(): lax.all_to_all(values, 'head', split_axis=1, concat_axis=0, tiled=True)  16 us
    all_to_all x1, blocking collectives, shards(): lax.all_to_all(outputs, 'head', split_axis=0, concat_axis=1, tiled=True)  15.2 us
    unnamed x1, blocking collectives  9.44 us
  transfers between devices with their start and end apart: 3, of which 3 were waited for; matrix products, arithmetic and copies ran while one was open for 1% of the time, Pallas kernels for 0%

profile of v5, /device:TPU:0, one launch (start us, length us, event | category | flops | bytes accessed | tf_op | source)
XLA Modules:
  0.0 214.6 jit_solution(7730825202787769719)
XLA Ops:
  6.5 0.0 copy-start.1
  6.5 0.0 all-gather.3.cloned.1.call-start
  6.5 1.3 copy.24
  7.9 0.0 copy-start.2
  7.9 16.9 %all_to_all.73 = bf16[288,4,384]{2,0,1:T(8,128)(2,1)} all-to-all(bf16[288,4,384]{2,0,1:T(8,128)(2,1)S(1)} %bitcast.49), channel_id=1, replica_groups=mesh['clips'=2,'ctx'=4,'head'=4] {'head'}, dimensions={1} | all-to-all | bytes 1769472 | tf_op jit(solution)/shard_map/all_to_all | solution.py:79
  24.8 0.0 all-gather.3.cloned.1.call-update
  24.9 0.0 all-gather.5.cloned.1.call-start
  24.9 0.0 copy-done.1
  24.9 0.1 copy.23
  25.0 0.0 copy-start.5
  25.0 0.0 copy-start.4
  25.0 0.0 copy-start.3
  25.1 16.0 %all_to_all.74 = bf16[288,4,384]{2,0,1:T(8,128)(2,1)} all-to-all(bf16[288,4,384]{2,0,1:T(8,128)(2,1)S(1)} %bitcast.50), channel_id=1, replica_groups=mesh['clips'=2,'ctx'=4,'head'=4] {'head'}, dimensions={1} | all-to-all | bytes 1769472 | tf_op jit(solution)/shard_map/all_to_all | solution.py:86
  41.0 0.0 all-gather.5.cloned.1.call-update
  41.0 0.0 copy-done.2
  41.0 1.0 copy.25
  42.0 3.5 %all-to-all-start = ((bf16[288,4,384]{2,0,1:T(8,128)(2,1)}), bf16[288,4,384]{2,0,1:T(8,128)(2,1)S(1)}, u32[]{:S(2)}, u32[]{:S(2)}) async-start(bf16[288,4,384]{2,0,1:T(8,128)(2,1)} %bitcast.27), calls=%async_computation | async-start | bytes 1769472 | tf_op jit(solution)/shard_map/all_to_all | solution.py:109
  45.6 0.0 copy-done.5
  45.6 0.7 dynamic-slice
  46.9 0.0 copy-done.4
  47.0 0.2 dynamic-update-slice
  47.2 9.4 %all-reduce.counts_ref = s32[12]{0:T(128)S(1)} all-reduce(s32[12]{0:T(128)S(1)} %dynamic-update-slice), channel_id=1, replica_groups=mesh['clips'=2,'ctx'=4,'head'=4] {'ctx'}, use_global_device_ids=true, to_apply=%add | all-reduce | flops 12 | bytes 96
  56.6 0.0 copy-done.3
  56.6 1.6 all-to-all-done
  58.2 37.7 %all-gather.3.cloned.1.call-done = bf16[4608,384]{1,0:T(8,128)(2,1)} async-done(((bf16[1152,384]{1,0:T(8,128)(2,1)}), bf16[4608,384]{1,0:T(8,128)(2,1)}) %all-gather.3.cloned.1.call-update) | async-done | bytes 3538960 | tf_op jit(solution)/shard_map/all_gather | solution.py:85
  95.9 70.1 %all-gather.5.cloned.1.call-done = bf16[4608,384]{1,0:T(8,128)(2,1)} async-done(((bf16[1152,384]{1,0:T(8,128)(2,1)}), bf16[4608,384]{1,0:T(8,128)(2,1)}) %all-gather.5.cloned.1.call-update) | async-done | bytes 3538960 | tf_op jit(solution)/shard_map/all_gather | solution.py:87
  166.0 0.0 copy-start
  166.0 2.0 copy-done
  168.0 23.6 %shard_map.55 = bf16[3,384,384]{2,1,0:T(8,128)(2,1)S(1)} custom-call(s32[3,8]{1,0:T(4,128)S(1)} %broadcast_clamp_fusion.lists_ref, s32[12]{0:T(128)S(1)} %all-reduce.counts_ref, bf16[3,384,384]{2,1,0:T(8,128)(2,1)S(1)} %bitcast.36, bf16[12,384,384]{2,1,0:T(8,128)(2,1)S(1)} %bitcast.28, bf16[12,384,384]{2,1,0:T(8,128)(2,1)S(1)} %bitcast.29, ...), custom_call_target="tpu_custom_call" | custom-call | tf_op jit(solution)/shard_map/pallas_call | solution.py:67
  191.6 15.2 %all_to_all.75 = bf16[4,288,384]{2,1,0:T(8,128)(2,1)S(1)} all-to-all(bf16[4,288,384]{2,1,0:T(8,128)(2,1)S(1)} %bitcast.37), channel_id=1, replica_groups=mesh['clips'=2,'ctx'=4,'head'=4] {'head'}, dimensions={0} | all-to-all | bytes 1769472 | tf_op jit(solution)/shard_map/all_to_all | solution.py:113
  206.8 1.0 copy.19
  (2 shorter events, 0.0 us)
Async XLA Ops:
  6.5 18.4 %copy-start.1 = (bf16[288,1536]{1,0:T(8,128)(2,1)S(1)}, bf16[288,1536]{1,0:T(8,128)(2,1)}, u32[]{:S(2)}) copy-start(bf16[288,1536]{1,0:T(8,128)(2,1)} %param.7) | copy-start | bytes 2654212
  6.5 89.3 %all-gather.3.cloned.1.call-start = ((), (), s32[]{:S(2)}) async-start(), calls=%async_computation.4 | async-start | bytes 4423680 | tf_op jit(solution)/shard_map/all_gather | solution.py:85
  7.9 33.2 %copy-start.2 = (bf16[288,1536]{1,0:T(8,128)(2,1)S(1)}, bf16[288,1536]{1,0:T(8,128)(2,1)}, u32[]{:S(2)}) copy-start(bf16[288,1536]{1,0:T(8,128)(2,1)} %param.5) | copy-start | bytes 2654212
  24.9 141.1 %all-gather.5.cloned.1.call-start = ((), (), s32[]{:S(2)}) async-start(), calls=%async_computation.5 | async-start | bytes 4423680 | tf_op jit(solution)/shard_map/all_gather | solution.py:87
  25.0 20.5 %copy-start.5 = (u32[32]{0:T(128)S(1)}, u32[32]{0:T(128)}, u32[]{:S(2)}) copy-start(u32[32]{0:T(128)} %constant.8) | copy-start | bytes 388
  25.0 21.9 %copy-start.4 = (s32[3]{0:T(128)S(1)}, s32[3]{0:T(128)}, u32[]{:S(2)}) copy-start(s32[3]{0:T(128)} %param.9) | copy-start | bytes 40
  25.0 31.6 %copy-start.3 = (s32[3,8]{1,0:T(4,128)S(1)}, s32[3,8]{1,0:T(4,128)}, u32[]{:S(2)}) copy-start(s32[3,8]{1,0:T(4,128)} %param.8) | copy-start | bytes 292
  42.0 16.2 %all-to-all-start = ((bf16[288,4,384]{2,0,1:T(8,128)(2,1)}), bf16[288,4,384]{2,0,1:T(8,128)(2,1)S(1)}, u32[]{:S(2)}, u32[]{:S(2)}) async-start(bf16[288,4,384]{2,0,1:T(8,128)(2,1)} %bitcast.27), calls=%async_computation | async-start | bytes 1769472 | tf_op jit(solution)/shard_map/all_to_all | solution.py:109
  166.0 2.0 copy-start
Sparse Core Ops, SparseCore 0:
  25.0 70.8 all-gather.2
  97.4 68.4 all-gather.4

commit v6 on v3

--- a/solution.py
+++ b/solution.py
@@ -24,7 +24,7 @@
     out_ref = refs[2 * NB]
     tile = pl.program_id(0)
     query_rows = query_ref[...]
-    slot_index = lax.broadcasted_iota(jnp.int32, (TILE, TILE), 1)
+    slot_index = lax.broadcasted_iota(jnp.int32, (1, TILE), 1)
     scores = []
     for entry in range(NB):
         part = lax.dot_general(

time: 212 us -> 212 us (level)
  no operation moved by 1% of the time
where the time goes in v6:
time: 212 us; the launch traced here: 211 us
  waiting for transfers between devices  110 us (52%)
  blocking collectives  53.8 us (25%)
  Pallas kernels  22.9 us (11%)
  between operations  14.1 us (7%)
  local copies, waits for them, and re-layouts  6.34 us (3%)
  starting transfers between devices  3.51 us (2%)
    all_gather x1, waiting for transfers between devices, shards(): ext_kv = lax.all_gather(block_kv, 'ctx', axis=0, tiled=True)  110 us
    all_to_all x1, blocking collectives, shards(): lax.all_to_all(paired, 'head', split_axis=1, concat_axis=0, tiled=True)  26.3 us
    pallas_call x1, Pallas kernels, attend(): pl.pallas_call(attend_kernel, grid_spec=spec, out_shape=jax.ShapeDtypeStr...  22.9 us
    all_to_all x1, blocking collectives, shards(): lax.all_to_all(outputs, 'head', split_axis=0, concat_axis=1, tiled=True)  15.2 us
    unnamed x1, blocking collectives  12.3 us
  transfers between devices with their start and end apart: 2, of which 1 were waited for; matrix products, arithmetic and copies ran while one was open for 1% of the time, Pallas kernels for 0%

profile of v6, /device:TPU:0, one launch (start us, length us, event | category | flops | bytes accessed | tf_op | source)
XLA Modules:
  0.0 211.4 jit_solution(4339548432249398738)
XLA Ops:
  6.5 0.0 copy-start
  6.5 0.0 all-gather.2.cloned.1.call-start
  6.5 1.9 reshape.26
  8.5 0.0 copy-done
  8.5 0.2 reshape.27
  8.7 0.8 pad_maximum_fusion
  9.4 0.2 copy.12
  9.7 26.3 %all_to_all.50 = bf16[288,4,768]{2,0,1:T(8,128)(2,1)} all-to-all(bf16[288,4,768]{2,0,1:T(8,128)(2,1)S(1)} %copy.12), channel_id=1, replica_groups=mesh['clips'=2,'ctx'=4,'head'=4] {'head'}, dimensions={1} | all-to-all | bytes 3538944 | tf_op jit(solution)/shard_map/all_to_all | solution.py:82
  36.0 0.0 copy-start.1
  36.0 0.0 all-gather.2.cloned.1.call-update
  36.0 1.1 copy-done.1
  37.1 0.0 copy-start.4
  37.1 0.0 copy-start.3
  37.1 0.0 copy-start.2
  37.1 1.0 copy.17
  38.1 3.5 %all-to-all-start = ((bf16[288,4,384]{2,0,1:T(8,128)(2,1)}), bf16[288,4,384]{2,0,1:T(8,128)(2,1)S(1)}, u32[]{:S(2)}, u32[]{:S(2)}) async-start(bf16[288,4,384]{2,0,1:T(8,128)(2,1)} %bitcast.17), calls=%async_computation | async-start | bytes 1769472 | tf_op jit(solution)/shard_map/all_to_all | solution.py:106
  41.7 0.0 copy-done.4
  41.7 0.6 dynamic-slice
  42.9 0.0 copy-done.3
  42.9 0.2 dynamic-update-slice
  43.2 12.3 %all-reduce.counts_ref = s32[12]{0:T(128)S(1)} all-reduce(s32[12]{0:T(128)S(1)} %dynamic-update-slice), channel_id=1, replica_groups=mesh['clips'=2,'ctx'=4,'head'=4] {'ctx'}, use_global_device_ids=true, to_apply=%add | all-reduce | flops 12 | bytes 96
  55.5 0.0 copy-done.2
  55.5 0.0 all-to-all-done
  55.5 109.9 %all-gather.2.cloned.1.call-done = bf16[4608,768]{1,0:T(8,128)(2,1)} async-done(((bf16[1152,768]{1,0:T(8,128)(2,1)}), bf16[4608,768]{1,0:T(8,128)(2,1)}) %all-gather.2.cloned.1.call-update) | async-done | bytes 7077904 | tf_op jit(solution)/shard_map/all_gather | solution.py:89
  165.4 22.9 %shard_map.55 = bf16[3,384,384]{2,1,0:T(8,128)(2,1)S(1)} custom-call(s32[3,8]{1,0:T(4,128)S(1)} %broadcast_clamp_fusion.lists_ref, s32[12]{0:T(128)S(1)} %all-reduce.counts_ref, bf16[3,384,384]{2,1,0:T(8,128)(2,1)S(1)} %bitcast.18, bf16[12,384,768]{2,1,0:T(8,128)(2,1)} %bitcast.20, bf16[12,384,768]{2,1,0:T(8,128)(2,1)} %bitcast.21, ...), custom_call_target="tpu_custom_call" | custom-call | tf_op jit(solution)/shard_map/pallas_call | solution.py:67
  188.3 15.2 %all_to_all.51 = bf16[4,288,384]{2,1,0:T(8,128)(2,1)S(1)} all-to-all(bf16[4,288,384]{2,1,0:T(8,128)(2,1)S(1)} %bitcast.19), channel_id=1, replica_groups=mesh['clips'=2,'ctx'=4,'head'=4] {'head'}, dimensions={0} | all-to-all | bytes 1769472 | tf_op jit(solution)/shard_map/all_to_all | solution.py:110
  203.5 1.0 copy.15
  (2 shorter events, 0.0 us)
Async XLA Ops:
  6.5 1.9 copy-start
  6.5 158.8 %all-gather.2.cloned.1.call-start = ((), (), s32[]{:S(2)}) async-start(), calls=%async_computation.3 | async-start | bytes 8847360 | tf_op jit(solution)/shard_map/all_gather | solution.py:89
  36.0 1.2 copy-start.1
  37.1 4.5 %copy-start.4 = (u32[32]{0:T(128)S(1)}, u32[32]{0:T(128)}, u32[]{:S(2)}) copy-start(u32[32]{0:T(128)} %constant.8) | copy-start | bytes 388
  37.1 5.8 %copy-start.3 = (s32[3]{0:T(128)S(1)}, s32[3]{0:T(128)}, u32[]{:S(2)}) copy-start(s32[3]{0:T(128)} %param.9) | copy-start | bytes 40
  37.1 18.3 %copy-start.2 = (s32[3,8]{1,0:T(4,128)S(1)}, s32[3,8]{1,0:T(4,128)}, u32[]{:S(2)}) copy-start(s32[3,8]{1,0:T(4,128)} %param.8) | copy-start | bytes 292
  38.1 17.3 %all-to-all-start = ((bf16[288,4,384]{2,0,1:T(8,128)(2,1)}), bf16[288,4,384]{2,0,1:T(8,128)(2,1)S(1)}, u32[]{:S(2)}, u32[]{:S(2)}) async-start(bf16[288,4,384]{2,0,1:T(8,128)(2,1)} %bitcast.17), calls=%async_computation | async-start | bytes 1769472 | tf_op jit(solution)/shard_map/all_to_all | solution.py:106
Sparse Core Ops, SparseCore 0:
  36.1 129.1 all-gather.1

commit v7 on v3

--- a/solution.py
+++ b/solution.py
@@ -86,8 +86,10 @@
     ctx_peers = lax.axis_size("ctx")
     if ctx_peers <= 2 * HOPS + 1:
         ext_tiles = ctx_peers * tiles_here
-        ext_kv = lax.all_gather(block_kv, "ctx", axis=0, tiled=True)
-        ext_counts = lax.all_gather(tile_counts, "ctx", axis=0, tiled=True)
+        pieces = jnp.stack([tile_counts // 16, tile_counts % 16], axis=1).astype(jnp.bfloat16)
+        ext_kv, pieces = lax.all_gather((block_kv, pieces), "ctx", axis=0, tiled=True)
+        pieces = pieces.astype(jnp.int32)
+        ext_counts = pieces[:, 0] * 16 + pieces[:, 1]
         first_tile = 0
     else:
         earlier = []

time: 212 us -> 212 us (level)
    unnamed x1 -> x0, blocking collectives: 12.3 us -> none
    all_gather x0 -> x1, blocking collectives: none -> 11.9 us  [shards(): lax.all_gather((block_kv, pieces), 'ctx', axis=0, tiled=True)]
  transfers between devices with their start and end apart: 2 -> 2, of which waited for: 1 -> 2; matrix products, arithmetic and copies ran while one was open for 1% -> 1% of each run, Pallas kernels for 0% -> 0%
where the time goes in v7:
time: 212 us; the launch traced here: 211 us
  waiting for transfers between devices  111 us (52%)
  blocking collectives  53.4 us (25%)
  Pallas kernels  22.9 us (11%)
  between operations  13.5 us (6%)
  local copies, waits for them, and re-layouts  5.79 us (3%)
  starting transfers between devices  3.51 us (2%)
    all_gather x1, waiting for transfers between devices, shards(): lax.all_gather((block_kv, pieces), 'ctx', axis=0, tiled=True)  111 us
    all_to_all x1, blocking collectives, shards(): lax.all_to_all(paired, 'head', split_axis=1, concat_axis=0, tiled=True)  26.3 us
    pallas_call x1, Pallas kernels, attend(): pl.pallas_call(attend_kernel, grid_spec=spec, out_shape=jax.ShapeDtypeStr...  22.9 us
    all_to_all x1, blocking collectives, shards(): lax.all_to_all(outputs, 'head', split_axis=0, concat_axis=1, tiled=True)  15.2 us
    all_gather x1, blocking collectives, shards(): lax.all_gather((block_kv, pieces), 'ctx', axis=0, tiled=True)  11.9 us
  transfers between devices with their start and end apart: 2, of which 2 were waited for; matrix products, arithmetic and copies ran while one was open for 1% of the time, Pallas kernels for 0%

profile of v7, /device:TPU:0, one launch (start us, length us, event | category | flops | bytes accessed | tf_op | source)
XLA Modules:
  0.0 211.2 jit_solution(12622742226547967553)
XLA Ops:
  6.5 0.0 copy-start
  6.5 0.0 all-gather.3.cloned.1.call-start
  6.5 1.9 reshape.29
  8.5 0.0 copy-done
  8.5 0.2 reshape.30
  8.7 0.8 pad_maximum_fusion
  9.4 0.2 copy.24
  9.7 26.3 %all_to_all.50 = bf16[288,4,768]{2,0,1:T(8,128)(2,1)} all-to-all(bf16[288,4,768]{2,0,1:T(8,128)(2,1)S(1)} %copy.24), channel_id=1, replica_groups=mesh['clips'=2,'ctx'=4,'head'=4] {'head'}, dimensions={1} | all-to-all | bytes 3538944 | tf_op jit(solution)/shard_map/all_to_all | solution.py:82
  36.0 0.0 copy-start.1
  36.0 0.0 all-gather.3.cloned.1.call-update
  36.0 1.1 copy-done.1
  37.1 0.0 copy-start.3
  37.1 0.0 copy-start.2
  37.1 1.0 copy.29
  38.1 3.5 %all-to-all-start = ((bf16[288,4,384]{2,0,1:T(8,128)(2,1)}), bf16[288,4,384]{2,0,1:T(8,128)(2,1)S(1)}, u32[]{:S(2)}, u32[]{:S(2)}) async-start(bf16[288,4,384]{2,0,1:T(8,128)(2,1)} %bitcast.26), calls=%async_computation | async-start | bytes 1769472 | tf_op jit(solution)/shard_map/all_to_all | solution.py:108
  41.7 0.0 copy-done.3
  41.7 11.9 %all-gather = bf16[4,3,2]{1,2,0:T(2,128)(2,1)S(1)} all-gather(bf16[1,3,2]{1,2,0:T(2,128)(2,1)S(1)} %maximum_bitcast_fusion), channel_id=1, replica_groups=mesh['clips'=2,'ctx'=4,'head'=4] {'ctx'}, dimensions={0}, use_global_device_ids=true | all-gather | bytes 60 | tf_op jit(solution)/shard_map/all_gather | solution.py:90
  53.6 0.1 copy.21
  53.7 0.1 copy.22
  53.8 0.1 reshape.35
  53.9 0.0 copy-done.2
  53.9 0.3 all-to-all-done
  54.3 110.9 %all-gather.3.cloned.1.call-done = bf16[4608,768]{1,0:T(8,128)(2,1)} async-done(((bf16[1152,768]{1,0:T(8,128)(2,1)}), bf16[4608,768]{1,0:T(8,128)(2,1)}) %all-gather.3.cloned.1.call-update) | async-done | bytes 7077904 | tf_op jit(solution)/shard_map/all_gather | solution.py:90
  165.2 22.9 %shard_map.55 = bf16[3,384,384]{2,1,0:T(8,128)(2,1)S(1)} custom-call(s32[3,8]{1,0:T(4,128)S(1)} %broadcast_clamp_fusion.lists_ref, s32[12]{0:T(128)S(1)} %add_bitcast_fusion.counts_ref, bf16[3,384,384]{2,1,0:T(8,128)(2,1)S(1)} %bitcast.27, bf16[12,384,768]{2,1,0:T(8,128)(2,1)} %bitcast.29, bf16[12,384,768]{2,1,0:T(8,128)(2,1)} %bitcast.30, ...), custom_call_target="tpu_custom_call" | custom-call | tf_op jit(solution)/shard_map/pallas_call | solution.py:67
  188.2 15.2 %all_to_all.51 = bf16[4,288,384]{2,1,0:T(8,128)(2,1)S(1)} all-to-all(bf16[4,288,384]{2,1,0:T(8,128)(2,1)S(1)} %bitcast.28), channel_id=1, replica_groups=mesh['clips'=2,'ctx'=4,'head'=4] {'head'}, dimensions={0} | all-to-all | bytes 1769472 | tf_op jit(solution)/shard_map/all_to_all | solution.py:112
  203.4 1.0 copy.27
  (5 shorter events, 0.0 us)
Async XLA Ops:
  6.5 1.9 copy-start
  6.5 158.7 %all-gather.3.cloned.1.call-start = ((), (), s32[]{:S(2)}) async-start(), calls=%async_computation.3 | async-start | bytes 8847360 | tf_op jit(solution)/shard_map/all_gather | solution.py:90
  36.0 1.2 copy-start.1
  37.1 4.5 %copy-start.3 = (s32[3]{0:T(128)S(1)}, s32[3]{0:T(128)}, u32[]{:S(2)}) copy-start(s32[3]{0:T(128)} %param.9) | copy-start | bytes 40
  37.1 16.8 %copy-start.2 = (s32[3,8]{1,0:T(4,128)S(1)}, s32[3,8]{1,0:T(4,128)}, u32[]{:S(2)}) copy-start(s32[3,8]{1,0:T(4,128)} %param.8) | copy-start | bytes 292
  38.1 16.2 %all-to-all-start = ((bf16[288,4,384]{2,0,1:T(8,128)(2,1)}), bf16[288,4,384]{2,0,1:T(8,128)(2,1)S(1)}, u32[]{:S(2)}, u32[]{:S(2)}) async-start(bf16[288,4,384]{2,0,1:T(8,128)(2,1)} %bitcast.26), calls=%async_computation | async-start | bytes 1769472 | tf_op jit(solution)/shard_map/all_to_all | solution.py:108
Sparse Core Ops, SparseCore 0:
  36.1 129.0 all-gather.2
